TPU v7x, 512 devices: a whole 4x4x16 slice. The times are simulated.
512 devices in a mesh: dp: 128 (over x, z, core), mp: 4 (over y).
Axes of the slice: x: 4, y: 4, z: 16, core: 2. Of those that a mesh axis runs over, the one named last changes fastest.
Arguments:
- media: bfloat16 [1024, 256, 1536], P('dp', None, 'mp'), may hold values from -24 to 24
- time_table: bfloat16 [8, 1536], P(None, 'mp'), may hold values from -4 to 4
- doc_images: int32 [256], P('dp'), may hold values from 0 to 8, as said below
- plan: int32 [128, 8], P('dp'), may hold values from -1 to 19, as said below
- latents: bfloat16 [64, 1536], replicated, may hold values from -6 to 6
- queries: bfloat16 [64, 1024], P(None, 'mp'), may hold values from -450 to 450
- key_weight: bfloat16 [1536, 1024], P(None, 'mp'), may hold values from -0.15625 to 0.15625
- value_weight: bfloat16 [1536, 1024], P(None, 'mp'), may hold values from -0.15625 to 0.15625
- out_weight: bfloat16 [1024, 1536], P('mp'), may hold values from -0.1875 to 0.1875
- cotangent: bfloat16 [512, 64, 1536], P('dp', None, 'mp'), may hold values from -6 to 6
Outputs:
- resampled: bfloat16 [512, 64, 1536], P('dp', None, 'mp')
- key_grad: float32 [1536, 1024], P('dp', 'mp')
- value_grad: float32 [1536, 1024], P('dp', 'mp')
Inputs may be any that keep to these rules, and one draw needn't show every extreme that they name: `doc_images`: A device's documents fill its image slots from slot 0 in document order and hold 8 images or fewer together; some document holds exactly 8. `plan`: entry s of device d's row is -1 exactly when slot s holds no image, else k * 4 + w with k from 0 to 4 and d + k a device of dp: the image goes to work slot w of device d + k. Each work slot receives at most one image; a device sends at most one image for each k from 1 to 4; some device sends one for every such k and fills its own 4 work slots.
All inputs are finite; a program needn't handle non-finite values.
Results may differ from a plain program's by a relative error of at most 0.0096.
Values may be sent and summed in bfloat16 or wider, within the bound.
A program may use at most 64 MiB of HBM per device.

v0:
```python
import jax
import jax.numpy as jnp
from jax import lax
from jax.sharding import Mesh
from jax.sharding import PartitionSpec as P

HEAD = 64
DP = ("dp_0", "dp_1", "dp_2")


norm_epsilon = 1e-05


def from_behind(block, axis, distance):
    devices = range(lax.axis_size(axis))
    route = [(i - distance, i) for i in devices if i - distance in devices]
    return lax.ppermute(block, axis, route)


def in_one_piece(arrays, axis, dim, along):
    both = jnp.concatenate(arrays, axis=along)
    whole, at, gathered = (lax.all_gather(both, axis, axis=dim, tiled=True), 0, [])
    for a in arrays:
        gathered.append(lax.slice_in_dim(whole, at, at + a.shape[along], axis=along))
        at += a.shape[along]
    return tuple(gathered)


def in_blocks(x, dim, size):
    shape = x.shape
    pieces = x.reshape(*shape[:dim], size, shape[dim] // size, *shape[dim + 1 :])
    return jnp.moveaxis(pieces, dim, 0)


def summed_on_arrival(x, axis, dim):
    size = lax.axis_size(axis)
    pieces = lax.all_to_all(in_blocks(x, dim, size), axis, 0, 0, tiled=True)
    return jnp.sum(pieces.astype(jnp.float32), axis=0)


def sum_in_two_steps(x, axes, dim):
    far, near = axes
    own = summed_on_arrival(in_blocks(x, dim, lax.axis_size(far)), near, dim + 1)
    return jnp.sum(
        lax.all_to_all(own.astype(jnp.bfloat16), far, 0, 0, tiled=True).astype(jnp.float32), axis=0
    )


def layer_norm(rows_in):
    average = jnp.mean(rows_in, axis=-1, keepdims=True)
    centred = rows_in - average
    spread = jnp.mean(centred * centred, axis=-1, keepdims=True)
    return centred * lax.rsqrt(spread + norm_epsilon)


def local(
    media,
    time_table,
    doc_images,
    plan,
    latents,
    queries,
    key_weight,
    value_weight,
    out_weight,
    cotangent,
):
    slot_cap = media.shape[0]
    image_tokens = media.shape[1]
    quarter = media.shape[2]
    work_slots = cotangent.shape[0]
    latent_count = cotangent.shape[1]
    reach_steps = slot_cap - work_slots
    model_width = latents.shape[1]
    inner_dev = queries.shape[1]
    head_count = inner_dev // HEAD
    context_rows = image_tokens + latent_count
    slot_iota = jnp.arange(slot_cap, dtype=jnp.int32)
    doc_ends = jnp.cumsum(doc_images)
    starts = doc_ends - doc_images
    start_of = jnp.max(jnp.where(starts[None, :] <= slot_iota[:, None], starts[None, :], 0), axis=1)
    position = slot_iota - start_of
    position_hot = (position[:, None] == slot_iota[None, :]).astype(jnp.bfloat16)
    time_rows = jnp.dot(position_hot, time_table, preferred_element_type=jnp.float32)
    framed = (media.astype(jnp.float32) + time_rows[:, None, :]).astype(jnp.bfloat16)
    plan_codes = plan[0]
    is_live = plan_codes >= 0
    helper = jnp.where(is_live, plan_codes // work_slots, -1)
    target = jnp.where(is_live, plan_codes % work_slots, -1)
    target_hot = (target[:, None] == jnp.arange(work_slots, dtype=jnp.int32)[None, :]) & is_live[
        :, None
    ]
    local_map = (target_hot & (helper == 0)[:, None]).astype(jnp.bfloat16)
    work_rows = jnp.einsum("sw,std->wtd", local_map, framed, preferred_element_type=jnp.float32)
    alive_slot = jnp.sum(local_map.astype(jnp.float32), axis=0)
    for offset in range(1, reach_steps + 1):
        chosen = (target_hot & (helper == offset)[:, None]).astype(jnp.bfloat16)
        picked = jnp.sum(chosen, axis=1)
        image_block = jnp.einsum(
            "s,std->td", picked, framed, preferred_element_type=jnp.float32
        ).astype(jnp.bfloat16)
        slot_mark = jnp.sum(chosen, axis=0)
        got_block, got_mark = from_behind((image_block, slot_mark), DP, offset)
        work_rows = (
            work_rows
            + got_mark.astype(jnp.float32)[:, None, None]
            * got_block.astype(jnp.float32)[None, :, :]
        )
        alive_slot = alive_slot + got_mark.astype(jnp.float32)
    work_media = work_rows.astype(jnp.bfloat16)
    full_media, cot_full = in_one_piece((work_media, cotangent), "mp", 2, 1)
    normed = layer_norm(full_media.astype(jnp.float32)).astype(jnp.bfloat16)
    normed_flat = normed.reshape(work_slots * image_tokens, model_width)
    latent_norm = layer_norm(latents.astype(jnp.float32)).astype(jnp.bfloat16)
    media_keys = (
        jnp.dot(normed_flat, key_weight, preferred_element_type=jnp.float32)
        .astype(jnp.bfloat16)
        .reshape(work_slots, image_tokens, inner_dev)
    )
    media_values = (
        jnp.dot(normed_flat, value_weight, preferred_element_type=jnp.float32)
        .astype(jnp.bfloat16)
        .reshape(work_slots, image_tokens, inner_dev)
    )
    latent_keys = jnp.dot(latent_norm, key_weight, preferred_element_type=jnp.float32).astype(
        jnp.bfloat16
    )
    latent_values = jnp.dot(latent_norm, value_weight, preferred_element_type=jnp.float32).astype(
        jnp.bfloat16
    )
    key_rows = jnp.concatenate(
        [media_keys, jnp.broadcast_to(latent_keys[None], (work_slots, latent_count, inner_dev))], 1
    )
    value_rows = jnp.concatenate(
        [
            media_values,
            jnp.broadcast_to(latent_values[None], (work_slots, latent_count, inner_dev)),
        ],
        1,
    )
    key_heads = key_rows.reshape(work_slots, context_rows, head_count, HEAD)
    value_heads = value_rows.reshape(work_slots, context_rows, head_count, HEAD)
    query_heads = queries.reshape(latent_count, head_count, HEAD)
    scores = (
        jnp.einsum("qhe,wkhe->whqk", query_heads, key_heads, preferred_element_type=jnp.float32)
        * 0.125
    )
    attention = jax.nn.softmax(scores, axis=-1)
    attention_b = attention.astype(jnp.bfloat16)
    attended = jnp.einsum(
        "whqk,wkhe->wqhe", attention_b, value_heads, preferred_element_type=jnp.float32
    ).astype(jnp.bfloat16)
    attended_flat = attended.reshape(work_slots * latent_count, inner_dev)
    partial_out = jnp.dot(attended_flat, out_weight, preferred_element_type=jnp.float32).reshape(
        work_slots, latent_count, model_width
    )
    summed_heads = summed_on_arrival(partial_out.astype(jnp.bfloat16), "mp", 2)
    latent_part = lax.dynamic_slice_in_dim(
        latents, lax.axis_index("mp") * quarter, quarter, 1
    ).astype(jnp.float32)
    resampled = ((latent_part[None] + summed_heads) * alive_slot[:, None, None]).astype(
        jnp.bfloat16
    )
    cot_live = cot_full * alive_slot.astype(jnp.bfloat16)[:, None, None]
    grad_attended = lax.dot_general(
        cot_live.reshape(work_slots * latent_count, model_width),
        out_weight,
        (((1,), (1,)), ((), ())),
        preferred_element_type=jnp.float32,
    ).astype(jnp.bfloat16)
    grad_heads = grad_attended.reshape(work_slots, latent_count, head_count, HEAD)
    grad_weights = jnp.einsum(
        "wqhe,wkhe->whqk", grad_heads, value_heads, preferred_element_type=jnp.float32
    )
    row_dot = jnp.sum(attention * grad_weights, axis=-1, keepdims=True)
    grad_scores = attention * (grad_weights - row_dot)
    grad_keys = (
        (
            jnp.einsum(
                "whqk,qhe->wkhe",
                grad_scores,
                query_heads.astype(jnp.float32),
                precision=lax.Precision.HIGHEST,
            )
            * 0.125
        )
        .astype(jnp.bfloat16)
        .reshape(work_slots, context_rows, inner_dev)
    )
    grad_values = (
        jnp.einsum("whqk,wqhe->wkhe", attention_b, grad_heads, preferred_element_type=jnp.float32)
        .astype(jnp.bfloat16)
        .reshape(work_slots, context_rows, inner_dev)
    )
    media_grads = jnp.concatenate(
        [grad_keys[:, :image_tokens], grad_values[:, :image_tokens]], 2
    ).reshape(work_slots * image_tokens, 2 * inner_dev)
    latent_grads = jnp.concatenate(
        [
            jnp.sum(grad_keys[:, image_tokens:].astype(jnp.float32), axis=0),
            jnp.sum(grad_values[:, image_tokens:].astype(jnp.float32), axis=0),
        ],
        1,
    )
    latent_norm32 = latent_norm.astype(jnp.float32)
    inverse_slots = 1.0 / (lax.axis_size(DP) * work_slots)
    media_part = lax.dot_general(
        normed_flat, media_grads, (((0,), (0,)), ((), ())), preferred_element_type=jnp.float32
    )
    latent_term = lax.dot_general(
        latent_norm32,
        latent_grads,
        (((0,), (0,)), ((), ())),
        precision=lax.Precision.HIGHEST,
        preferred_element_type=jnp.float32,
    )
    shares = sum_in_two_steps(
        ((media_part + latent_term) * inverse_slots).astype(jnp.bfloat16),
        (("dp_0", "dp_1"), "dp_2"),
        0,
    )
    return (resampled, shares[:, :inner_dev], shares[:, inner_dev:])


def solution(mesh):
    finer = Mesh(mesh.devices.reshape(4, 16, 2, mesh.shape["mp"]), ("dp_0", "dp_1", "dp_2", "mp"))
    return jax.shard_map(
        local,
        mesh=finer,
        in_specs=(
            P(DP, None, "mp"),
            P(None, "mp"),
            P(DP),
            P(DP, None),
            P(),
            P(None, "mp"),
            P(None, "mp"),
            P(None, "mp"),
            P("mp", None),
            P(DP, None, "mp"),
        ),
        out_specs=(P(DP, None, "mp"), P(DP, "mp"), P(DP, "mp")),
        check_vma=False,
    )
```

profile of v0, /device:TPU:1, one launch (start us, length us, event | category | flops | bytes accessed | tf_op | source)
XLA Modules:
  0.0 261.7 jit_solution(7394261875260566753)
XLA Ops:
  7.2 0.7 fusion.74
  8.0 0.7 broadcast_compare_fusion.4
  8.6 0.8 reduce-window.9
  9.4 0.7 bitcast_subtract_fusion
  10.2 0.9 fusion.55
  11.1 1.7 add_convert_fusion
  13.1 1.1 fusion.29
  14.2 4.9 %collective-permute-start.1 = (bf16[256,384]{1,0:T(8,128)(2,1)S(1)}, bf16[256,384]{1,0:T(8,128)(2,1)S(1)}, u32[]{:S(2)}, u32[]{:S(2)}) collective-permute-start(bf16[256,384]{1,0:T(8,128)(2,1)S(1)} %bitcast.116), channel_id=1, source_target_pairs={{0,4},{4,8},{8,12},{12,16},{16,20},{20,24},{24,28},{28,32},{32,36}... | collective-permute-start | bytes 589832 | tf_op jit(solution)/shard_map/ppermute | solution.py:17
  19.1 1.1 fusion.27
  20.3 3.6 %collective-permute-start.3 = (bf16[256,384]{1,0:T(8,128)(2,1)S(1)}, bf16[256,384]{1,0:T(8,128)(2,1)S(1)}, u32[]{:S(2)}, u32[]{:S(2)}) collective-permute-start(bf16[256,384]{1,0:T(8,128)(2,1)S(1)} %bitcast.117), channel_id=1, source_target_pairs={{0,8},{4,12},{8,16},{12,20},{16,24},{20,28},{24,32},{28,36},{32,40... | collective-permute-start | bytes 589832 | tf_op jit(solution)/shard_map/ppermute | solution.py:17
  23.8 1.1 fusion.25
  24.9 3.7 %collective-permute-start.5 = (bf16[256,384]{1,0:T(8,128)(2,1)S(1)}, bf16[256,384]{1,0:T(8,128)(2,1)S(1)}, u32[]{:S(2)}, u32[]{:S(2)}) collective-permute-start(bf16[256,384]{1,0:T(8,128)(2,1)S(1)} %bitcast.118), channel_id=1, source_target_pairs={{0,12},{4,16},{8,20},{12,24},{16,28},{20,32},{24,36},{28,40},{32,4... | collective-permute-start | bytes 589832 | tf_op jit(solution)/shard_map/ppermute | solution.py:17
  28.6 1.1 fusion.23
  29.8 6.1 %collective-permute-start.7 = (bf16[256,384]{1,0:T(8,128)(2,1)S(1)}, bf16[256,384]{1,0:T(8,128)(2,1)S(1)}, u32[]{:S(2)}, u32[]{:S(2)}) collective-permute-start(bf16[256,384]{1,0:T(8,128)(2,1)S(1)} %bitcast.119), channel_id=1, source_target_pairs={{0,16},{4,20},{8,24},{12,28},{16,32},{20,36},{24,40},{28,44},{32,4... | collective-permute-start | bytes 589832 | tf_op jit(solution)/shard_map/ppermute | solution.py:17
  35.9 4.1 %collective-permute-start = (bf16[4]{0:T(256)(128)(2,1)S(1)}, bf16[4]{0:T(256)(128)(2,1)S(1)}, u32[]{:S(2)}, u32[]{:S(2)}) collective-permute-start(bf16[4]{0:T(256)(128)(2,1)S(1)} %get-tuple-element.3), channel_id=1, source_target_pairs={{0,4},{4,8},{8,12},{12,16},{16,20},{20,24},{24,28},{28,32},{32,36}... | collective-permute-start | bytes 32 | tf_op jit(solution)/shard_map/ppermute | solution.py:17
  40.1 1.2 collective-permute-done
  41.4 7.8 %collective-permute-start.6 = (bf16[4]{0:T(256)(128)(2,1)S(1)}, bf16[4]{0:T(256)(128)(2,1)S(1)}, u32[]{:S(2)}, u32[]{:S(2)}) collective-permute-start(bf16[4]{0:T(256)(128)(2,1)S(1)} %get-tuple-element.12), channel_id=1, source_target_pairs={{0,16},{4,20},{8,24},{12,28},{16,32},{20,36},{24,40},{28,44},{32,4... | collective-permute-start | bytes 32 | tf_op jit(solution)/shard_map/ppermute | solution.py:17
  49.3 0.7 collective-permute-done.6
  49.9 8.2 %collective-permute-start.4 = (bf16[4]{0:T(256)(128)(2,1)S(1)}, bf16[4]{0:T(256)(128)(2,1)S(1)}, u32[]{:S(2)}, u32[]{:S(2)}) collective-permute-start(bf16[4]{0:T(256)(128)(2,1)S(1)} %get-tuple-element.14), channel_id=1, source_target_pairs={{0,12},{4,16},{8,20},{12,24},{16,28},{20,32},{24,36},{28,40},{32,4... | collective-permute-start | bytes 32 | tf_op jit(solution)/shard_map/ppermute | solution.py:17
  58.2 0.7 collective-permute-done.4
  58.9 2.1 collective-permute-start.2
  61.7 2.7 %add_convert_fusion.1 = bf16[4,256,384]{2,0,1:T(4,128)(2,1)S(1)} fusion(f32[256,384]{1,0:T(8,128)S(1)} %convert_element_type.181, f32[4]{0:T(128)S(1)} %convert_element_type.179, f32[256,384]{1,0:T(8,128)S(1)} %convert_element_type.177, f32[4]{0:T(128)S(1)} %convert_element_type.175, f32[256,384]{1,0:T(8,128)S(1)} %convert_element_type.173, ...), kind=kOutput, calls=%fused_computation.23 | convolution fusion | flops 9830432 | bytes 3932264 | tf_op jit(solution)/shard_map/sw,std->wtd/dot_general | solution.py:94
  64.4 1.6 pad_maximum_fusion
  67.8 60.9 %all-gather.2.cloned.1.call-done = bf16[4,320,1536]{2,0,1:T(4,128)(2,1)} async-done(((bf16[4,320,384]{2,0,1:T(4,128)(2,1)}), bf16[4,320,1536]{2,0,1:T(4,128)(2,1)}) %all-gather.2.cloned.1.call-update) | async-done | bytes 3932176 | tf_op jit(solution)/shard_map/all_gather | solution.py:22
  128.8 3.3 %convert_reduce_fusion = f32[4,256]{0,1:T(8,128)S(1)} fusion(bf16[4,320,1536]{2,0,1:T(4,128)(2,1)} %all-gather.2.cloned.1.call-done), kind=kLoop, calls=%fused_computation.2 | loop fusion | flops 3144704 | bytes 3149824 | tf_op jit(solution)/shard_map/reduce_sum | solution.py:50
  132.1 5.0 %fusion.3 = f32[4,256]{0,1:T(8,128)S(1)} fusion(f32[4,256]{0,1:T(8,128)S(1)} %broadcast_multiply_fusion, bf16[4,320,1536]{2,0,1:T(4,128)(2,1)} %all-gather.2.cloned.1.call-done), kind=kLoop, calls=%fused_computation.5 | loop fusion | flops 6290432 | bytes 3153920 | tf_op jit(solution)/shard_map/reduce_sum | solution.py:52
  137.2 2.0 fusion.4
  139.8 1.1 copy-done.2
  140.8 1.0 convolution_convert_fusion.2
  141.8 1.8 convolution_convert_fusion.3
  146.4 0.9 copy.137
  147.3 1.8 fusion.97
  149.2 1.9 multiply_reduce_fusion
  152.5 1.3 fusion.17
  154.7 1.0 copy.212
  155.9 3.8 %convolution_bitcast_fusion = f32[1536,512]{1,0:T(8,128)S(1)} fusion(bf16[4,256,256]{2,1,0:T(8,128)(2,1)S(1)} %copy.177, bf16[4,256,256]{2,1,0:T(8,128)(2,1)S(1)} %copy.176, bf16[4,256,1536]{2,0,1:T(4,128)(2,1)} %copy-done.2), kind=kOutput, calls=%fused_computation.9 | convolution fusion | flops 1612709888 | bytes 7340032 | tf_op jit(solution)/shard_map/dot_general | solution.py:207
  159.7 2.9 %fusion.6 = bf16[1536,512]{1,0:T(8,128)(2,1)} fusion(f32[1536,512]{1,0:T(8,128)S(1)} %convolution_bitcast_fusion, f32[64,256]{0,1:T(8,128)S(1)} %get-tuple-element.35, f32[64,256]{0,1:T(8,128)S(1)} %get-tuple-element.36, bf16[64,1536]{1,0:T(8,128)(2,1)S(1)} %copy-done.3, f32[64]{0:T(128)S(1)} %add_rsqrt_fusion.1, f32[64]{0:T(128)S(1)} %broadcast_multiply_fusion.1), kind=kOutput, calls=%fused_computation.11 | convolution fusion | flops 606765056 | bytes 5046784 | tf_op jit(solution)/shard_map/dot_general | solution.py:210
  162.6 2.4 reshape_reshape.3
  165.0 0.9 copy.153
  165.8 6.7 %all_to_all.15 = bf16[2,64,12,512]{3,1,2,0:T(8,128)(2,1)S(1)} all-to-all(bf16[2,64,12,512]{3,1,2,0:T(8,128)(2,1)S(1)} %copy.153), channel_id=1, replica_groups=mesh['dp_0'=4,'dp_1'=16,'dp_2'=2,'mp'=4] {'dp_2'}, dimensions={0} | all-to-all | bytes 3145728 | tf_op jit(solution)/shard_map/all_to_all | solution.py:37
  172.5 4.2 %all-to-all-start = ((bf16[4,4,64,384]{3,2,1,0:T(8,128)(2,1)}), bf16[4,4,64,384]{3,2,1,0:T(8,128)(2,1)}, u32[]{:S(2)}, u32[]{:S(2)}) async-start(bf16[4,4,64,384]{3,2,1,0:T(8,128)(2,1)} %bitcast.98), calls=%async_computation | async-start | bytes 1572864 | tf_op jit(solution)/shard_map/all_to_all | solution.py:37
  177.3 1.4 copy.154
  178.7 10.0 %all-to-all-done = bf16[4,4,64,384]{3,2,1,0:T(8,128)(2,1)} async-done(((bf16[4,4,64,384]{3,2,1,0:T(8,128)(2,1)}), bf16[4,4,64,384]{3,2,1,0:T(8,128)(2,1)}, u32[]{:S(2)}, u32[]{:S(2)}) %all-to-all-start) | async-done | bytes 786464 | tf_op jit(solution)/shard_map/all_to_all | solution.py:37
  188.8 15.3 %all-to-all-start.2 = ((bf16[64,12,512]{2,1,0:T(8,128)(2,1)}), bf16[64,12,512]{2,1,0:T(8,128)(2,1)S(1)}, u32[]{:S(2)}, u32[]{:S(2)}) async-start(bf16[64,12,512]{2,1,0:T(8,128)(2,1)} %copy.154), calls=%async_computation.2 | async-start | bytes 2097152 | tf_op jit(solution)/shard_map/all_to_all | solution.py:45
  204.1 1.3 convert_reduce_fusion.2
  205.4 0.8 multiply_convert_fusion.1
  206.2 47.8 %all-to-all-done.2 = bf16[64,12,512]{2,1,0:T(8,128)(2,1)S(1)} async-done(((bf16[64,12,512]{2,1,0:T(8,128)(2,1)}), bf16[64,12,512]{2,1,0:T(8,128)(2,1)S(1)}, u32[]{:S(2)}, u32[]{:S(2)}) %all-to-all-start.2) | async-done | bytes 786464 | tf_op jit(solution)/shard_map/all_to_all | solution.py:45
  254.2 0.6 fusion.96
  (79 shorter events, 9.8 us)
Async XLA Ops:
  7.2 137.0 %copy-start = (bf16[256,1536]{1,0:T(8,128)(2,1)S(1)}, bf16[256,1536]{1,0:T(8,128)(2,1)}, u32[]{:S(2)}) copy-start(bf16[256,1536]{1,0:T(8,128)(2,1)} %param.18) | copy-start | bytes 2359300
  7.2 121.6 %all-gather.2.cloned.1.call-start = ((), (), s32[]{:S(2)}) async-start(), calls=%async_computation.3 | async-start | bytes 4915200 | tf_op jit(solution)/shard_map/all_gather | solution.py:22
  14.2 47.3 %collective-permute-start.1 = (bf16[256,384]{1,0:T(8,128)(2,1)S(1)}, bf16[256,384]{1,0:T(8,128)(2,1)S(1)}, u32[]{:S(2)}, u32[]{:S(2)}) collective-permute-start(bf16[256,384]{1,0:T(8,128)(2,1)S(1)} %bitcast.116), channel_id=1, source_target_pairs={{0,4},{4,8},{8,12},{12,16},{16,20},{20,24},{24,28},{28,32},{32,36}... | collective-permute-start | bytes 589832 | tf_op jit(solution)/shard_map/ppermute | solution.py:17
  20.3 41.3 %collective-permute-start.3 = (bf16[256,384]{1,0:T(8,128)(2,1)S(1)}, bf16[256,384]{1,0:T(8,128)(2,1)S(1)}, u32[]{:S(2)}, u32[]{:S(2)}) collective-permute-start(bf16[256,384]{1,0:T(8,128)(2,1)S(1)} %bitcast.117), channel_id=1, source_target_pairs={{0,8},{4,12},{8,16},{12,20},{16,24},{20,28},{24,32},{28,36},{32,40... | collective-permute-start | bytes 589832 | tf_op jit(solution)/shard_map/ppermute | solution.py:17
  24.9 15.1 %copy-start.7 = (bf16[4,64,384]{2,1,0:T(8,128)(2,1)S(1)}, bf16[4,64,384]{2,1,0:T(8,128)(2,1)}, u32[]{:S(2)}) copy-start(bf16[4,64,384]{2,1,0:T(8,128)(2,1)} %param.19) | copy-start | bytes 589828
  24.9 36.6 %collective-permute-start.5 = (bf16[256,384]{1,0:T(8,128)(2,1)S(1)}, bf16[256,384]{1,0:T(8,128)(2,1)S(1)}, u32[]{:S(2)}, u32[]{:S(2)}) collective-permute-start(bf16[256,384]{1,0:T(8,128)(2,1)S(1)} %bitcast.118), channel_id=1, source_target_pairs={{0,12},{4,16},{8,20},{12,24},{16,28},{20,32},{24,36},{28,40},{32,4... | collective-permute-start | bytes 589832 | tf_op jit(solution)/shard_map/ppermute | solution.py:17
  29.8 31.9 %collective-permute-start.7 = (bf16[256,384]{1,0:T(8,128)(2,1)S(1)}, bf16[256,384]{1,0:T(8,128)(2,1)S(1)}, u32[]{:S(2)}, u32[]{:S(2)}) collective-permute-start(bf16[256,384]{1,0:T(8,128)(2,1)S(1)} %bitcast.119), channel_id=1, source_target_pairs={{0,16},{4,20},{8,24},{12,28},{16,32},{20,36},{24,40},{28,44},{32,4... | collective-permute-start | bytes 589832 | tf_op jit(solution)/shard_map/ppermute | solution.py:17
  35.9 5.5 %collective-permute-start = (bf16[4]{0:T(256)(128)(2,1)S(1)}, bf16[4]{0:T(256)(128)(2,1)S(1)}, u32[]{:S(2)}, u32[]{:S(2)}) collective-permute-start(bf16[4]{0:T(256)(128)(2,1)S(1)} %get-tuple-element.3), channel_id=1, source_target_pairs={{0,4},{4,8},{8,12},{12,16},{16,20},{20,24},{24,28},{28,32},{32,36}... | collective-permute-start | bytes 32 | tf_op jit(solution)/shard_map/ppermute | solution.py:17
  41.4 8.6 %collective-permute-start.6 = (bf16[4]{0:T(256)(128)(2,1)S(1)}, bf16[4]{0:T(256)(128)(2,1)S(1)}, u32[]{:S(2)}, u32[]{:S(2)}) collective-permute-start(bf16[4]{0:T(256)(128)(2,1)S(1)} %get-tuple-element.12), channel_id=1, source_target_pairs={{0,16},{4,20},{8,24},{12,28},{16,32},{20,36},{24,40},{28,44},{32,4... | collective-permute-start | bytes 32 | tf_op jit(solution)/shard_map/ppermute | solution.py:17
  49.9 8.9 %collective-permute-start.4 = (bf16[4]{0:T(256)(128)(2,1)S(1)}, bf16[4]{0:T(256)(128)(2,1)S(1)}, u32[]{:S(2)}, u32[]{:S(2)}) collective-permute-start(bf16[4]{0:T(256)(128)(2,1)S(1)} %get-tuple-element.14), channel_id=1, source_target_pairs={{0,12},{4,16},{8,20},{12,24},{16,28},{20,32},{24,36},{28,40},{32,4... | collective-permute-start | bytes 32 | tf_op jit(solution)/shard_map/ppermute | solution.py:17
  58.9 2.6 %collective-permute-start.2 = (bf16[4]{0:T(256)(128)(2,1)S(1)}, bf16[4]{0:T(256)(128)(2,1)S(1)}, u32[]{:S(2)}, u32[]{:S(2)}) collective-permute-start(bf16[4]{0:T(256)(128)(2,1)S(1)} %get-tuple-element.16), channel_id=1, source_target_pairs={{0,8},{4,12},{8,16},{12,20},{16,24},{20,28},{24,32},{28,36},{32,40... | collective-permute-start | bytes 32 | tf_op jit(solution)/shard_map/ppermute | solution.py:17
  64.4 1.7 copy-start.3
  64.4 2.0 copy-start.4
  66.0 1.1 copy-start.5
  66.0 1.6 copy-start.8
  128.8 8.4 %copy-start.1 = (bf16[4,320,1536]{2,0,1:T(4,128)(2,1)S(1)}, bf16[4,320,1536]{2,0,1:T(4,128)(2,1)}, u32[]{:S(2)}) copy-start(bf16[4,320,1536]{2,0,1:T(4,128)(2,1)} %all-gather.2.cloned.1.call-done) | copy-start | bytes 11796484
  139.2 1.7 copy-start.2
  144.0 1.0 copy-start.6
  151.1 1.4 copy-start.9
  172.5 16.3 %all-to-all-start = ((bf16[4,4,64,384]{3,2,1,0:T(8,128)(2,1)}), bf16[4,4,64,384]{3,2,1,0:T(8,128)(2,1)}, u32[]{:S(2)}, u32[]{:S(2)}) async-start(bf16[4,4,64,384]{3,2,1,0:T(8,128)(2,1)} %bitcast.98), calls=%async_computation | async-start | bytes 1572864 | tf_op jit(solution)/shard_map/all_to_all | solution.py:37
  188.8 65.2 %all-to-all-start.2 = ((bf16[64,12,512]{2,1,0:T(8,128)(2,1)}), bf16[64,12,512]{2,1,0:T(8,128)(2,1)S(1)}, u32[]{:S(2)}, u32[]{:S(2)}) async-start(bf16[64,12,512]{2,1,0:T(8,128)(2,1)} %copy.154), calls=%async_computation.2 | async-start | bytes 2097152 | tf_op jit(solution)/shard_map/all_to_all | solution.py:45
Sparse Core Ops, SparseCore 0:
  66.2 62.5 all-gather.1
where the time goes:
time: 266 us; the launch traced here: 262 us
  waiting for transfers between devices  122 us (46%)
  starting transfers between devices  60.1 us (23%)
  matrix products  24.6 us (9%)
  other arithmetic  20.8 us (8%)
  between operations  14.6 us (5%)
  local copies, waits for them, and re-layouts  13 us (5%)
  blocking collectives  6.66 us (3%)
    all_gather x1, waiting for transfers between devices, in_one_piece(): lax.all_gather(both, axis, axis=dim, tiled=True)  60.9 us
    all_to_all x1, waiting for transfers between devices, sum_in_two_steps(): lax.all_to_all(own.astype(jnp.bfloat16), far, 0, 0, tiled=True)  47.8 us
    ppermute x8, starting transfers between devices, from_behind(): return lax.ppermute(block, axis, route)  40.5 us
    all_to_all x1, starting transfers between devices, sum_in_two_steps(): lax.all_to_all(own.astype(jnp.bfloat16), far, 0, 0, tiled=True)  15.3 us
    all_to_all x1, waiting for transfers between devices, summed_on_arrival(): pieces = lax.all_to_all(in_blocks(x, dim, size), axis, 0, 0, tiled=True)  10 us
    all_to_all x1, blocking collectives, summed_on_arrival(): pieces = lax.all_to_all(in_blocks(x, dim, size), axis, 0, 0, tiled=True)  6.66 us
  transfers between devices with their start and end apart: 11, of which 7 were waited for; matrix products, arithmetic and copies ran while one was open for 3% of the time, Pallas kernels for 0%

commit v1 on v0

--- a/solution.py
+++ b/solution.py
@@ -1,29 +1,250 @@
+import functools
+
 import jax
 import jax.numpy as jnp
 from jax import lax
-from jax.sharding import Mesh
+from jax.experimental import pallas as pl
+from jax.experimental.pallas import tpu as pltpu
 from jax.sharding import PartitionSpec as P
 
 HEAD = 64
-DP = ("dp_0", "dp_1", "dp_2")
-
+MESH = pl.DeviceIdType.MESH
+CHUNKS = 4
+REACH = 4
 
 norm_epsilon = 1e-05
 
 
-def from_behind(block, axis, distance):
-    devices = range(lax.axis_size(axis))
-    route = [(i - distance, i) for i in devices if i - distance in devices]
-    return lax.ppermute(block, axis, route)
-
-
-def in_one_piece(arrays, axis, dim, along):
-    both = jnp.concatenate(arrays, axis=along)
-    whole, at, gathered = (lax.all_gather(both, axis, axis=dim, tiled=True), 0, [])
-    for a in arrays:
-        gathered.append(lax.slice_in_dim(whole, at, at + a.shape[along], axis=along))
-        at += a.shape[along]
-    return tuple(gathered)
+def plan_scalars(plan_ref, docs_ref, slots, work):
+    far_slot = [jnp.int32(0)] * (REACH + 1)
+    far_work = [jnp.int32(-1)] * (REACH + 1)
+    own_slot = [jnp.int32(0)] * work
+    own_live = [jnp.int32(0)] * work
+    for s in range(slots):
+        code = plan_ref[0, s]
+        for k in range(1, REACH + 1):
+            inside = (code >= k * work) & (code < (k + 1) * work)
+            far_slot[k] = jnp.where(inside, s, far_slot[k])
+            far_work[k] = jnp.where(inside, code - k * work, far_work[k])
+        for w in range(work):
+            own_slot[w] = jnp.where(code == w, s, own_slot[w])
+            own_live[w] = jnp.where(code == w, 1, own_live[w])
+    first = docs_ref[0]
+
+    def position(s):
+        return s - jnp.where(s >= first, first, 0)
+
+    return far_slot, far_work, own_slot, own_live, position
+
+
+def gather_body(
+    n_dp,
+    n_mp,
+    plan_ref,
+    docs_ref,
+    media_ref,
+    time_ref,
+    cot_ref,
+    full_ref,
+    alive_ref,
+    send_buf,
+    head_buf,
+    got_buf,
+    got_head,
+    far_send,
+    far_recv,
+    head_send,
+    head_recv,
+    ring_send,
+    ring_recv,
+):
+    slots, tokens, quarter = media_ref.shape
+    work = cot_ref.shape[0]
+    rows = tokens // CHUNKS
+    half = work // 2
+    me_d = lax.axis_index("dp")
+    me_m = lax.axis_index("mp")
+
+    def far(k):
+        return lax.rem(me_d + (k + n_dp), n_dp)
+
+    right, left = lax.rem(me_m + 1, n_mp), lax.rem(me_m + n_mp - 1, n_mp)
+    opposite = lax.rem(me_m + 2, n_mp)
+    barrier = pltpu.get_barrier_semaphore()
+    for k in range(1, REACH + 1):
+        for to in (far(k), far(-k)):
+            pl.semaphore_signal(
+                barrier, inc=1, device_id={"dp": to, "mp": me_m}, device_id_type=MESH
+            )
+    for to in (right, left):
+        pl.semaphore_signal(barrier, inc=1, device_id={"dp": me_d, "mp": to}, device_id_type=MESH)
+
+    far_slot, far_work, own_slot, own_live, position = plan_scalars(
+        plan_ref, docs_ref, slots, work
+    )
+    times = time_ref[...].astype(jnp.float32)
+    time_rows = lax.broadcasted_iota(jnp.int32, times.shape, 0)
+
+    def time_of(s):
+        return jnp.sum(jnp.where(time_rows == position(s), times, 0.0), axis=0, keepdims=True)
+
+    mark_rows = lax.broadcasted_iota(jnp.int32, head_buf.shape[1:], 0)
+    for k in range(1, REACH + 1):
+        head_buf[k - 1] = jnp.where(mark_rows == far_work[k], 1.0, 0.0).astype(jnp.bfloat16)
+        row = time_of(far_slot[k])
+        for c in range(CHUNKS):
+            send_buf[c, k - 1] = (
+                media_ref[far_slot[k], c * rows : (c + 1) * rows, :].astype(jnp.float32) + row
+            ).astype(jnp.bfloat16)
+    own_rows = [time_of(own_slot[w]) for w in range(work)]
+
+    pl.semaphore_wait(barrier, 2 * REACH + 2)
+
+    def ring_copy(src, dst, i, to):
+        return pltpu.make_async_remote_copy(
+            src_ref=src,
+            dst_ref=dst,
+            send_sem=ring_send.at[i],
+            recv_sem=ring_recv.at[i],
+            device_id={"dp": me_d, "mp": to},
+            device_id_type=MESH,
+        )
+
+    def own_sends(c, src):
+        return [
+            ring_copy(src, full_ref.at[me_m, c], 4 * c, right),
+            ring_copy(src, full_ref.at[me_m, c], 4 * c + 1, left),
+        ]
+
+    def own_arrivals(c):
+        return [
+            ring_copy(full_ref.at[left, c], full_ref.at[left, c], 4 * c, right),
+            ring_copy(full_ref.at[right, c], full_ref.at[right, c], 4 * c + 1, left),
+        ]
+
+    def forwards(c):
+        first = full_ref.at[left, c, pl.ds(0, half)]
+        second = full_ref.at[right, c, pl.ds(half, half)]
+        return [
+            ring_copy(first, first, 4 * c + 2, right),
+            ring_copy(second, second, 4 * c + 3, left),
+        ]
+
+    def forward_arrivals(c):
+        first = full_ref.at[opposite, c, pl.ds(0, half)]
+        second = full_ref.at[opposite, c, pl.ds(half, half)]
+        return [
+            ring_copy(first, first, 4 * c + 2, right),
+            ring_copy(second, second, 4 * c + 3, left),
+        ]
+
+    def far_copy(c, k):
+        return pltpu.make_async_remote_copy(
+            src_ref=send_buf.at[c, k - 1],
+            dst_ref=got_buf.at[c, k - 1],
+            send_sem=far_send.at[c, k - 1],
+            recv_sem=far_recv.at[c, k - 1],
+            device_id={"dp": far(k), "mp": me_m},
+            device_id_type=MESH,
+        )
+
+    def head_copy(k):
+        return pltpu.make_async_remote_copy(
+            src_ref=head_buf.at[k - 1],
+            dst_ref=got_head.at[k - 1],
+            send_sem=head_send.at[k - 1],
+            recv_sem=head_recv.at[k - 1],
+            device_id={"dp": far(k), "mp": me_m},
+            device_id_type=MESH,
+        )
+
+    started = own_sends(CHUNKS, cot_ref)
+    for copy in started:
+        copy.start()
+    for k in range(REACH, 0, -1):
+        head_copy(k).start()
+    for c in range(CHUNKS):
+        for k in range(REACH, 0, -1):
+            far_copy(c, k).start()
+    full_ref[me_m, CHUNKS] = cot_ref[...]
+
+    for k in range(1, REACH + 1):
+        head_copy(k).wait_recv()
+    marks = [got_head[k].astype(jnp.float32) for k in range(REACH)]
+    lives = [jnp.where(own_live[w] == 1, 1.0, 0.0) for w in range(work)]
+    for w in range(work):
+        total = marks[0][w : w + 1, :128]
+        for k in range(1, REACH):
+            total = total + marks[k][w : w + 1, :128]
+        alive_ref[w : w + 1, :] = total + lives[w]
+
+    def place(c):
+        for k in range(1, REACH + 1):
+            far_copy(c, k).wait_recv()
+        for w in range(work):
+            block = media_ref[own_slot[w], c * rows : (c + 1) * rows, :].astype(jnp.float32)
+            block = (block + own_rows[w]) * lives[w]
+            for k in range(REACH):
+                block = block + marks[k][w : w + 1, :] * got_buf[c, k].astype(jnp.float32)
+            full_ref[me_m, c, w] = block.astype(jnp.bfloat16)
+        copies = own_sends(c, full_ref.at[me_m, c])
+        for copy in copies:
+            copy.start()
+        return copies
+
+    order = [CHUNKS] + list(range(CHUNKS))
+    for i, c in enumerate(order):
+        if i < CHUNKS:
+            started += place(i)
+        for copy in own_arrivals(c):
+            copy.wait_recv()
+        for copy in forwards(c):
+            copy.start()
+            started.append(copy)
+    for c in order:
+        for copy in forward_arrivals(c):
+            copy.wait_recv()
+    for copy in started:
+        copy.wait_send()
+    for k in range(1, REACH + 1):
+        head_copy(k).wait_send()
+        for c in range(CHUNKS):
+            far_copy(c, k).wait_send()
+
+
+def gather(n_dp, n_mp, plan, docs, media, times, cot):
+    slots, tokens, quarter = media.shape
+    work, latent_count = cot.shape[:2]
+    rows = tokens // CHUNKS
+    bf16 = jnp.bfloat16
+    vmem = pl.BlockSpec(memory_space=pltpu.VMEM)
+    smem = pl.BlockSpec(memory_space=pltpu.SMEM)
+    dma = pltpu.SemaphoreType.DMA
+    return pl.pallas_call(
+        functools.partial(gather_body, n_dp, n_mp),
+        name="route_and_gather",
+        out_shape=(
+            jax.ShapeDtypeStruct((n_mp, CHUNKS + 1, work, rows, quarter), bf16),
+            jax.ShapeDtypeStruct((8, 128), jnp.float32),
+        ),
+        in_specs=[smem, smem, vmem, vmem, vmem],
+        out_specs=(vmem, vmem),
+        scratch_shapes=[
+            pltpu.VMEM((CHUNKS, REACH, rows, quarter), bf16),
+            pltpu.VMEM((REACH, 16, quarter), bf16),
+            pltpu.VMEM((CHUNKS, REACH, rows, quarter), bf16),
+            pltpu.VMEM((REACH, 16, quarter), bf16),
+            dma((CHUNKS, REACH)),
+            dma((CHUNKS, REACH)),
+            dma((REACH,)),
+            dma((REACH,)),
+            dma((4 * CHUNKS + 4,)),
+            dma((4 * CHUNKS + 4,)),
+        ],
+        compiler_params=pltpu.CompilerParams(
+            collective_id=0, has_side_effects=True, vmem_limit_bytes=48 << 20
+        ),
+    )(plan, docs, media, times, cot)
 
 
 def in_blocks(x, dim, size):
@@ -65,50 +286,19 @@
     out_weight,
     cotangent,
 ):
-    slot_cap = media.shape[0]
     image_tokens = media.shape[1]
     quarter = media.shape[2]
     work_slots = cotangent.shape[0]
     latent_count = cotangent.shape[1]
-    reach_steps = slot_cap - work_slots
     model_width = latents.shape[1]
     inner_dev = queries.shape[1]
     head_count = inner_dev // HEAD
     context_rows = image_tokens + latent_count
-    slot_iota = jnp.arange(slot_cap, dtype=jnp.int32)
-    doc_ends = jnp.cumsum(doc_images)
-    starts = doc_ends - doc_images
-    start_of = jnp.max(jnp.where(starts[None, :] <= slot_iota[:, None], starts[None, :], 0), axis=1)
-    position = slot_iota - start_of
-    position_hot = (position[:, None] == slot_iota[None, :]).astype(jnp.bfloat16)
-    time_rows = jnp.dot(position_hot, time_table, preferred_element_type=jnp.float32)
-    framed = (media.astype(jnp.float32) + time_rows[:, None, :]).astype(jnp.bfloat16)
-    plan_codes = plan[0]
-    is_live = plan_codes >= 0
-    helper = jnp.where(is_live, plan_codes // work_slots, -1)
-    target = jnp.where(is_live, plan_codes % work_slots, -1)
-    target_hot = (target[:, None] == jnp.arange(work_slots, dtype=jnp.int32)[None, :]) & is_live[
-        :, None
-    ]
-    local_map = (target_hot & (helper == 0)[:, None]).astype(jnp.bfloat16)
-    work_rows = jnp.einsum("sw,std->wtd", local_map, framed, preferred_element_type=jnp.float32)
-    alive_slot = jnp.sum(local_map.astype(jnp.float32), axis=0)
-    for offset in range(1, reach_steps + 1):
-        chosen = (target_hot & (helper == offset)[:, None]).astype(jnp.bfloat16)
-        picked = jnp.sum(chosen, axis=1)
-        image_block = jnp.einsum(
-            "s,std->td", picked, framed, preferred_element_type=jnp.float32
-        ).astype(jnp.bfloat16)
-        slot_mark = jnp.sum(chosen, axis=0)
-        got_block, got_mark = from_behind((image_block, slot_mark), DP, offset)
-        work_rows = (
-            work_rows
-            + got_mark.astype(jnp.float32)[:, None, None]
-            * got_block.astype(jnp.float32)[None, :, :]
-        )
-        alive_slot = alive_slot + got_mark.astype(jnp.float32)
-    work_media = work_rows.astype(jnp.bfloat16)
-    full_media, cot_full = in_one_piece((work_media, cotangent), "mp", 2, 1)
+    n_mp = lax.axis_size("mp")
+    full, alive = gather(lax.axis_size("dp"), n_mp, plan, doc_images, media, time_table, cotangent)
+    alive_slot = alive[:work_slots, 0]
+    whole = full.transpose(2, 1, 3, 0, 4).reshape(work_slots, image_tokens + latent_count, model_width)
+    full_media, cot_full = whole[:, :image_tokens], whole[:, image_tokens:]
     normed = layer_norm(full_media.astype(jnp.float32)).astype(jnp.bfloat16)
     normed_flat = normed.reshape(work_slots * image_tokens, model_width)
     latent_norm = layer_norm(latents.astype(jnp.float32)).astype(jnp.bfloat16)
@@ -203,7 +393,7 @@
         1,
     )
     latent_norm32 = latent_norm.astype(jnp.float32)
-    inverse_slots = 1.0 / (lax.axis_size(DP) * work_slots)
+    inverse_slots = 1.0 / (lax.axis_size("dp") * work_slots)
     media_part = lax.dot_general(
         normed_flat, media_grads, (((0,), (0,)), ((), ())), preferred_element_type=jnp.float32
     )
@@ -214,31 +404,26 @@
         precision=lax.Precision.HIGHEST,
         preferred_element_type=jnp.float32,
     )
-    shares = sum_in_two_steps(
-        ((media_part + latent_term) * inverse_slots).astype(jnp.bfloat16),
-        (("dp_0", "dp_1"), "dp_2"),
-        0,
-    )
+    shares = summed_on_arrival(((media_part + latent_term) * inverse_slots).astype(jnp.bfloat16), "dp", 0)
     return (resampled, shares[:, :inner_dev], shares[:, inner_dev:])
 
 
 def solution(mesh):
-    finer = Mesh(mesh.devices.reshape(4, 16, 2, mesh.shape["mp"]), ("dp_0", "dp_1", "dp_2", "mp"))
     return jax.shard_map(
         local,
-        mesh=finer,
+        mesh=mesh,
         in_specs=(
-            P(DP, None, "mp"),
+            P("dp", None, "mp"),
             P(None, "mp"),
-            P(DP),
-            P(DP, None),
+            P("dp"),
+            P("dp", None),
             P(),
             P(None, "mp"),
             P(None, "mp"),
             P(None, "mp"),
             P("mp", None),
-            P(DP, None, "mp"),
+            P("dp", None, "mp"),
         ),
-        out_specs=(P(DP, None, "mp"), P(DP, "mp"), P(DP, "mp")),
+        out_specs=(P("dp", None, "mp"), P("dp", "mp"), P("dp", "mp")),
         check_vma=False,
     )

time: 266 us -> 228 us (0.86); the launches traced: 262 us -> 227 us
  Pallas kernels: 0 us -> 52.6 us
  starting transfers between devices: 60.1 us -> 15.7 us
  waiting for transfers between devices: 122 us -> 97.1 us
  between operations: 14.6 us -> 1 us
  local copies, waits for them, and re-layouts: 13 us -> 26.4 us
  other arithmetic: 20.8 us -> 12.5 us
  blocking collectives: 6.66 us -> 0 us
  matrix products: 24.6 us -> 21.5 us
    all_to_all x1 -> x2, waiting for transfers between devices: 10 us -> 97.1 us  [summed_on_arrival(): pieces = lax.all_to_all(in_blocks(x, dim, size), axis, 0, 0, tiled=True)]
    all_gather x1 -> x0, waiting for transfers between devices: 60.9 us -> none  [in_one_piece(): lax.all_gather(both, axis, axis=dim, tiled=True)]
    pallas_call x0 -> x1, Pallas kernels: none -> 52.6 us  [gather(): pl.pallas_call(functools.partial(gather_body, n_dp, n_mp), name='route_an...]
    all_to_all x1 -> x0, waiting for transfers between devices: 47.8 us -> none  [sum_in_two_steps(): lax.all_to_all(own.astype(jnp.bfloat16), far, 0, 0, tiled=True)]
    ppermute x8 -> x0, starting transfers between devices: 40.5 us -> none  [from_behind(): return lax.ppermute(block, axis, route)]
    all_to_all x1 -> x0, starting transfers between devices: 15.3 us -> none  [sum_in_two_steps(): lax.all_to_all(own.astype(jnp.bfloat16), far, 0, 0, tiled=True)]
    all_to_all x1 -> x2, starting transfers between devices: 4.2 us -> 15.7 us  [summed_on_arrival(): pieces = lax.all_to_all(in_blocks(x, dim, size), axis, 0, 0, tiled=True)]
    dot_general x6 -> x0, matrix products: 7.93 us -> none  [the longest x4 4.31 us: local(): jnp.einsum('s,std->td', picked, framed, preferred_element_type=jnp.float32)]
  transfers between devices with their start and end apart: 11 -> 2, of which waited for: 7 -> 1; matrix products, arithmetic and copies ran while one was open for 3% -> 9% of each run, Pallas kernels for 0% -> 0%
where the time goes in v1:
time: 228 us; the launch traced here: 227 us
  waiting for transfers between devices  97.1 us (43%)
  Pallas kernels  52.6 us (23%)
  local copies, waits for them, and re-layouts  26.4 us (12%)
  matrix products  21.5 us (9%)
  starting transfers between devices  15.7 us (7%)
  other arithmetic  12.5 us (5%)
    all_to_all x2, waiting for transfers between devices, summed_on_arrival(): pieces = lax.all_to_all(in_blocks(x, dim, size), axis, 0, 0, tiled=True)  97.1 us
    pallas_call x1, Pallas kernels, gather(): pl.pallas_call(functools.partial(gather_body, n_dp, n_mp), name='route_an...  52.6 us
    all_to_all x2, starting transfers between devices, summed_on_arrival(): pieces = lax.all_to_all(in_blocks(x, dim, size), axis, 0, 0, tiled=True)  15.7 us
    reshape x1, local copies, waits for them, and re-layouts, local(): full.transpose(2, 1, 3, 0, 4)  7.32 us
    unnamed x30, local copies, waits for them, and re-layouts  6.05 us
    transpose x1, local copies, waits for them, and re-layouts, local(): full.transpose(2, 1, 3, 0, 4)  5.3 us
  transfers between devices with their start and end apart: 2, of which 1 were waited for; matrix products, arithmetic and copies ran while one was open for 9% of the time, Pallas kernels for 0%

profile of v1, /device:TPU:1, one launch (start us, length us, event | category | flops | bytes accessed | tf_op | source)
XLA Modules:
  0.0 226.7 jit_solution(12663079642880684797)
XLA Ops:
  0.7 1.2 convert_reduce_fusion.5
  1.9 1.2 fusion.34
  3.1 1.6 convolution_convert_fusion.6
  4.6 1.6 convolution_convert_fusion.7
  6.2 52.6 %route_and_gather.1 = (bf16[4,5,4,64,384]{4,3,2,1,0:T(8,128)(2,1)S(1)}, f32[8,128]{1,0:T(8,128)S(1)}) custom-call(s32[1,8]{1,0:T(1,128)S(1)} %copy-done.4, s32[2]{0:T(128)S(1)} %copy-done.5, bf16[8,256,384]{2,1,0:T(8,128)(2,1)S(1)} %copy-done.1, bf16[8,384]{1,0:T(8,128)(2,1)S(1)} %copy-done.3, bf16[4,64,384]{2,1,0:T(8,128)(2,1)S(1)} %copy-done.2), custom_call_target="tpu_custom_call" | custom-call | tf_op jit(solution)/shard_map/route_and_gather/pallas_call | solution.py:223
  58.9 5.3 %copy.47 = bf16[4,5,64,4,384]{4,3,2,1,0:T(4,128)(2,1)} copy(bf16[4,5,64,4,384]{4,2,0,1,3:T(8,128)(2,1)S(1)} %bitcast.48) | data formatting | bytes 7864320 | tf_op jit(solution)/shard_map/transpose | solution.py:300
  64.2 7.3 %reshape.88 = bf16[4,320,1536]{2,1,0:T(8,128)(2,1)} reshape(bf16[4,5,64,4,384]{4,3,2,1,0:T(4,128)(2,1)} %copy.47) | data formatting | bytes 7864320 | tf_op jit(solution)/shard_map/reshape | solution.py:300
  71.5 2.5 %convert_reduce_fusion = f32[4,256]{1,0:T(4,128)S(1)} fusion(bf16[4,320,1536]{2,1,0:T(8,128)(2,1)} %reshape.88), kind=kLoop, calls=%fused_computation.2 | loop fusion | flops 3144704 | bytes 3149824 | tf_op jit(solution)/shard_map/reduce_sum | solution.py:271
  74.0 2.9 %fusion.3 = f32[4,256]{1,0:T(4,128)S(1)} fusion(f32[4,256]{1,0:T(4,128)S(1)} %broadcast_multiply_fusion, bf16[4,320,1536]{2,1,0:T(8,128)(2,1)} %reshape.88), kind=kLoop, calls=%fused_computation.5 | loop fusion | flops 6290432 | bytes 3153920 | tf_op jit(solution)/shard_map/reduce_sum | solution.py:273
  76.9 0.9 fusion.4
  77.8 0.2 copy-done.11
  78.0 1.0 convolution_convert_fusion.2
  79.0 0.5 copy-done.8
  79.5 0.3 copy-done.12
  79.8 1.0 convolution_convert_fusion.3
  80.7 0.1 copy.80
  80.9 0.1 copy.77
  81.1 0.1 copy.73
  81.2 0.1 slice_reduce_fusion
  81.3 1.3 slice_multiply_fusion
  82.6 0.4 convolution_convert_fusion.5
  83.0 0.2 reshape.93
  83.2 0.4 reshape.102
  83.6 0.6 copy.53
  84.2 0.4 reshape.101
  84.7 0.5 copy.50
  85.3 1.8 fusion.58
  87.1 3.0 %multiply_reduce_fusion = (f32[4,4,64]{2,0,1:T(4,128)S(1)}, bf16[4,4,64,320]{3,2,0,1:T(8,128)(2,1)S(1)}, f32[4,4,64,320]{3,2,0,1:T(8,128)}) fusion(f32[4,4,64,320]{3,2,0,1:T(8,128)} %get-tuple-element.12, f32[4,4,64]{2,0,1:T(4,128)S(1)} %get-tuple-element.11, bf16[4,64,4,64]{3,2,1,0:T(4,128)(2,1)S(1)} %reshape.93, ...), kind=kOutput, calls=%fused_computation.20 | convolution fusion | flops 44563456 | bytes 4071424 | tf_op jit(solution)/shard_map/wqhe,wkhe->whqk/dot_general | solution.py:362
  90.1 0.4 convolution_convert_fusion.4
  90.5 0.4 convolution_convert_fusion
  91.0 1.0 copy.104
  92.0 3.7 %all-to-all-start = ((bf16[4,4,64,384]{3,2,1,0:T(8,128)(2,1)}), bf16[4,4,64,384]{3,2,1,0:T(8,128)(2,1)S(1)}, u32[]{:S(2)}, u32[]{:S(2)}) async-start(bf16[4,4,64,384]{3,2,1,0:T(8,128)(2,1)} %bitcast.47), calls=%async_computation | async-start | bytes 1572864 | tf_op jit(solution)/shard_map/all_to_all | solution.py:258
  95.7 1.5 convolution_convert_fusion.1
  97.2 3.1 %fusion.17 = bf16[4,320,4,64]{1,3,0,2:T(8,128)(2,1)S(1)} fusion(bf16[64,4,64,1]{0,2,3,1:T(8,128)(2,1)S(1)} %copy.73, f32[4,4,64,320]{3,2,0,1:T(8,128)} %get-tuple-element.13, f32[4,4,64]{2,0,1:T(4,128)S(1)} %get-tuple-element.7, f32[4,4,64,320]{3,2,0,1:T(8,128)} %get-tuple-element.12, f32[4,4,64]{2,0,1:T(4,128)S(1)} %get-tuple-element.11), kind=kOutput, calls=%fused_computation.25 | convolution fusion | flops 253296640 | bytes 3317760 | tf_op jit(solution)/shard_map/whqk,qhe->wkhe/dot_general | solution.py:369
  100.5 0.8 slice.38
  101.3 2.0 copy.86
  103.4 0.9 slice.39
  104.2 2.1 copy.87
  106.3 4.0 %convolution_bitcast_fusion = f32[1536,512]{1,0:T(8,128)S(1)} fusion(bf16[4,256,1536]{2,1,0:T(8,128)(2,1)} %copy-done.8, bf16[4,256,256]{2,1,0:T(8,128)(2,1)} %copy.87, bf16[4,256,256]{2,1,0:T(8,128)(2,1)} %copy.86), kind=kOutput, calls=%fused_computation.10 | convolution fusion | flops 1612709888 | bytes 7340032 | tf_op jit(solution)/shard_map/dot_general | solution.py:397
  110.4 1.7 fusion.6
  112.1 1.5 reshape.96
  113.7 0.9 copy-done.9
  114.6 12.0 %all-to-all-start.1 = ((bf16[128,12,512]{2,1,0:T(8,128)(2,1)}), bf16[128,12,512]{2,1,0:T(8,128)(2,1)S(1)}, u32[]{:S(2)}, u32[]{:S(2)}) async-start(bf16[128,12,512]{2,1,0:T(8,128)(2,1)} %reshape.96), calls=%async_computation.1 | async-start | bytes 4194304 | tf_op jit(solution)/shard_map/all_to_all | solution.py:258
  126.6 1.3 convert_reduce_fusion.2
  127.9 0.8 multiply_convert_fusion.1
  128.6 97.1 %all-to-all-done.1 = bf16[128,12,512]{2,1,0:T(8,128)(2,1)S(1)} async-done(((bf16[128,12,512]{2,1,0:T(8,128)(2,1)}), bf16[128,12,512]{2,1,0:T(8,128)(2,1)S(1)}, u32[]{:S(2)}, u32[]{:S(2)}) %all-to-all-start.1) | async-done | bytes 1572896 | tf_op jit(solution)/shard_map/all_to_all | solution.py:258
  225.7 0.4 convert_reduce_fusion.1
  226.1 0.6 fusion.57
  (36 shorter events, 0.5 us)
Async XLA Ops:
  0.6 82.0 %copy-start = (bf16[256,1536]{1,0:T(8,128)(2,1)S(1)}, bf16[256,1536]{1,0:T(8,128)(2,1)}, u32[]{:S(2)}) copy-start(bf16[256,1536]{1,0:T(8,128)(2,1)} %param.18) | copy-start | bytes 2359300
  0.6 5.5 %copy-start.2 = (bf16[4,64,384]{2,1,0:T(8,128)(2,1)S(1)}, bf16[4,64,384]{2,1,0:T(8,128)(2,1)}, u32[]{:S(2)}) copy-start(bf16[4,64,384]{2,1,0:T(8,128)(2,1)} %cot_ref.1) | copy-start | bytes 589828
  0.7 5.5 %copy-start.4 = (s32[1,8]{1,0:T(1,128)S(1)}, s32[1,8]{1,0:T(1,128)}, u32[]{:S(2)}) copy-start(s32[1,8]{1,0:T(1,128)} %plan_ref.1) | copy-start | bytes 100
  0.7 5.5 %copy-start.5 = (s32[2]{0:T(128)S(1)}, s32[2]{0:T(128)}, u32[]{:S(2)}) copy-start(s32[2]{0:T(128)} %docs_ref.1) | copy-start | bytes 28
  0.7 5.5 %copy-start.3 = (bf16[8,384]{1,0:T(8,128)(2,1)S(1)}, bf16[8,384]{1,0:T(8,128)(2,1)}, u32[]{:S(2)}) copy-start(bf16[8,384]{1,0:T(8,128)(2,1)} %time_ref.1) | copy-start | bytes 18436
  0.7 5.5 %copy-start.1 = (bf16[8,256,384]{2,1,0:T(8,128)(2,1)S(1)}, bf16[8,256,384]{2,1,0:T(8,128)(2,1)}, u32[]{:S(2)}) copy-start(bf16[8,256,384]{2,1,0:T(8,128)(2,1)} %media_ref.1) | copy-start | bytes 4718596
  71.5 5.4 %copy-start.6 = (bf16[4,320,1536]{2,1,0:T(8,128)(2,1)S(1)}, bf16[4,320,1536]{2,1,0:T(8,128)(2,1)}, u32[]{:S(2)}) copy-start(bf16[4,320,1536]{2,1,0:T(8,128)(2,1)} %reshape.88) | copy-start | bytes 11796484
  76.9 1.1 copy-start.11
  77.8 1.7 copy-start.8
  78.0 1.7 copy-start.12
  79.8 1.2 copy-start.13
  90.1 0.9 copy-start.10
  92.0 21.7 %all-to-all-start = ((bf16[4,4,64,384]{3,2,1,0:T(8,128)(2,1)}), bf16[4,4,64,384]{3,2,1,0:T(8,128)(2,1)S(1)}, u32[]{:S(2)}, u32[]{:S(2)}) async-start(bf16[4,4,64,384]{3,2,1,0:T(8,128)(2,1)} %bitcast.47), calls=%async_computation | async-start | bytes 1572864 | tf_op jit(solution)/shard_map/all_to_all | solution.py:258
  106.3 4.1 %copy-start.7 = (bf16[64,1536]{1,0:T(8,128)(2,1)S(1)}, bf16[64,1536]{1,0:T(8,128)(2,1)}, u32[]{:S(2)}) copy-start(bf16[64,1536]{1,0:T(8,128)(2,1)} %param.14) | copy-start | bytes 589828
  113.7 0.9 copy-start.9
  114.6 111.1 %all-to-all-start.1 = ((bf16[128,12,512]{2,1,0:T(8,128)(2,1)}), bf16[128,12,512]{2,1,0:T(8,128)(2,1)S(1)}, u32[]{:S(2)}, u32[]{:S(2)}) async-start(bf16[128,12,512]{2,1,0:T(8,128)(2,1)} %reshape.96), calls=%async_computation.1 | async-start | bytes 4194304 | tf_op jit(solution)/shard_map/all_to_all | solution.py:258

commit v2 on v1

--- a/solution.py
+++ b/solution.py
@@ -247,31 +247,414 @@
     )(plan, docs, media, times, cot)
 
 
-def in_blocks(x, dim, size):
-    shape = x.shape
-    pieces = x.reshape(*shape[:dim], size, shape[dim] // size, *shape[dim + 1 :])
-    return jnp.moveaxis(pieces, dim, 0)
-
-
-def summed_on_arrival(x, axis, dim):
-    size = lax.axis_size(axis)
-    pieces = lax.all_to_all(in_blocks(x, dim, size), axis, 0, 0, tiled=True)
-    return jnp.sum(pieces.astype(jnp.float32), axis=0)
-
-
-def sum_in_two_steps(x, axes, dim):
-    far, near = axes
-    own = summed_on_arrival(in_blocks(x, dim, lax.axis_size(far)), near, dim + 1)
-    return jnp.sum(
-        lax.all_to_all(own.astype(jnp.bfloat16), far, 0, 0, tiled=True).astype(jnp.float32), axis=0
+def attend_body(
+    full_ref,
+    alive_ref,
+    latents_ref,
+    queries_ref,
+    key_weight_ref,
+    value_weight_ref,
+    out_weight_ref,
+    partial_ref,
+    grads_ref,
+    context,
+    cot_live,
+    keys,
+    values,
+    grads,
+):
+    n_mp, chunks, work, rows, quarter = full_ref.shape
+    chunks = chunks - 1
+    tokens = chunks * rows
+    latent_count, width = latents_ref.shape
+    inner = queries_ref.shape[1]
+    heads = inner // HEAD
+    f32, bf16 = jnp.float32, jnp.bfloat16
+    contract_last = (((1,), (1,)), ((), ()))
+    contract_first = (((0,), (0,)), ((), ()))
+
+    def dot(a, b, dims=(((1,), (0,)), ((), ()))):
+        return lax.dot_general(a, b, dims, preferred_element_type=f32)
+
+    def normalise(parts):
+        parts = [p.astype(f32) for p in parts]
+        average = sum(jnp.sum(p, axis=-1, keepdims=True) for p in parts) * (1.0 / width)
+        parts = [p - average for p in parts]
+        spread = sum(jnp.sum(p * p, axis=-1, keepdims=True) for p in parts) * (1.0 / width)
+        scale = lax.rsqrt(spread + norm_epsilon)
+        return [(p * scale).astype(bf16) for p in parts]
+
+    latent_norm = normalise([latents_ref[...]])[0]
+    for w in range(work):
+        context[work * tokens + w * latent_count : work * tokens + (w + 1) * latent_count, :] = (
+            latent_norm
+        )
+    latent_keys = dot(latent_norm, key_weight_ref[...]).astype(bf16)
+    latent_values = dot(latent_norm, value_weight_ref[...]).astype(bf16)
+
+    def project(i, carry):
+        c, w = i // work, i % work
+        at = pl.multiple_of(w * tokens + c * rows, rows)
+        pieces = normalise([full_ref[m, c, w] for m in range(n_mp)])
+        for m in range(n_mp):
+            context[pl.ds(at, rows), m * quarter : (m + 1) * quarter] = pieces[m]
+        return carry
+
+    lax.fori_loop(0, chunks * work, project, 0)
+
+    def project_slot(w, carry):
+        at = pl.multiple_of(w * tokens, tokens)
+        normed = context[pl.ds(at, tokens), :]
+        keys[pl.ds(at, tokens), :] = dot(normed, key_weight_ref[...]).astype(bf16)
+        values[pl.ds(at, tokens), :] = dot(normed, value_weight_ref[...]).astype(bf16)
+        return carry
+
+    lax.fori_loop(0, work, project_slot, 0)
+
+    row_head = lax.broadcasted_iota(jnp.int32, (heads * latent_count, inner), 0) // latent_count
+    col_head = lax.broadcasted_iota(jnp.int32, (heads * latent_count, inner), 1) // HEAD
+    same_head = row_head == col_head
+
+    def spread_heads(x):
+        return jnp.where(same_head, jnp.concatenate([x.astype(f32)] * heads, axis=0), 0.0)
+
+    wide_queries32 = spread_heads(queries_ref[...])
+    wide_queries = wide_queries32.astype(bf16)
+    wide_queries_t = wide_queries32.T.astype(bf16)
+    latent_scores = dot(latent_keys, wide_queries, contract_last) * 0.125
+
+    for w in range(work):
+        alive = jnp.concatenate([alive_ref[w : w + 1, :]] * (quarter // 128), axis=1)
+        for m in range(n_mp):
+            cot_live[w * latent_count : (w + 1) * latent_count, m * quarter : (m + 1) * quarter] = (
+                full_ref[m, chunks, w].astype(f32) * alive
+            ).astype(bf16)
+    grad_attended = dot(cot_live[...], out_weight_ref[...], contract_last)
+
+    for w in range(work):
+        at = w * tokens
+        slot_keys = keys[at : at + tokens, :]
+        slot_values = values[at : at + tokens, :]
+        scores = dot(slot_keys, wide_queries, contract_last) * 0.125
+        top = jnp.maximum(
+            jnp.max(scores, axis=0, keepdims=True), jnp.max(latent_scores, axis=0, keepdims=True)
+        )
+        weight = jnp.exp(scores - top)
+        latent_weight = jnp.exp(latent_scores - top)
+        total = jnp.sum(weight, axis=0, keepdims=True) + jnp.sum(
+            latent_weight, axis=0, keepdims=True
+        )
+        attention = weight / total
+        latent_attention = latent_weight / total
+        attention_b = attention.astype(bf16)
+        latent_attention_b = latent_attention.astype(bf16)
+        attended = dot(attention_b, slot_values, contract_first) + dot(
+            latent_attention_b, latent_values, contract_first
+        )
+        attended = jnp.where(same_head, attended, 0.0)
+        attended = sum(
+            attended[h * latent_count : (h + 1) * latent_count, :] for h in range(heads)
+        ).astype(bf16)
+        partial = dot(attended, out_weight_ref[...]).astype(bf16)
+        for m in range(n_mp):
+            partial_ref[m, w] = partial[:, m * quarter : (m + 1) * quarter]
+
+        slot_grad = grad_attended[w * latent_count : (w + 1) * latent_count, :].astype(bf16)
+        wide_grad32 = spread_heads(slot_grad)
+        wide_grad = wide_grad32.astype(bf16)
+        wide_grad_t = wide_grad32.T.astype(bf16)
+        slope = dot(slot_values, wide_grad, contract_last)
+        latent_slope = dot(latent_values, wide_grad, contract_last)
+        row_dot = jnp.sum(attention * slope, axis=0, keepdims=True) + jnp.sum(
+            latent_attention * latent_slope, axis=0, keepdims=True
+        )
+        for where, count, att, att_b, slopes in (
+            (at, tokens, attention, attention_b, slope),
+            (work * tokens + w * latent_count, latent_count, latent_attention, latent_attention_b, latent_slope),
+        ):
+            grad_scores = att * (slopes - row_dot)
+            high = grad_scores.astype(bf16)
+            low = (grad_scores - high.astype(f32)).astype(bf16)
+            grad_keys = (
+                dot(wide_queries_t, high, contract_last) + dot(wide_queries_t, low, contract_last)
+            ) * 0.125
+            grads[0:inner, where : where + count] = grad_keys.astype(bf16)
+            grads[inner : 2 * inner, where : where + count] = dot(
+                wide_grad_t, att_b, contract_last
+            ).astype(bf16)
+
+    inverse = 1.0 / (n_mp_dp_slots(work))
+    for kind in range(2):
+        for m in range(n_mp):
+            grads_ref[kind, m] = (
+                dot(
+                    grads[kind * inner : (kind + 1) * inner, :],
+                    context[:, m * quarter : (m + 1) * quarter],
+                )
+                * inverse
+            ).astype(bf16)
+
+
+def n_mp_dp_slots(work):
+    return lax.axis_size("dp") * work
+
+
+def attend(full, alive, latents, queries, key_weight, value_weight, out_weight):
+    n_mp, parts, work, rows, quarter = full.shape
+    tokens = (parts - 1) * rows
+    latent_count, width = latents.shape
+    inner = queries.shape[1]
+    context_rows = work * (tokens + latent_count)
+    bf16 = jnp.bfloat16
+    vmem = pl.BlockSpec(memory_space=pltpu.VMEM)
+    return pl.pallas_call(
+        attend_body,
+        name="attend",
+        out_shape=(
+            jax.ShapeDtypeStruct((n_mp, work, latent_count, quarter), bf16),
+            jax.ShapeDtypeStruct((2, n_mp, inner, quarter), bf16),
+        ),
+        in_specs=[vmem] * 7,
+        out_specs=(vmem, vmem),
+        scratch_shapes=[
+            pltpu.VMEM((context_rows, width), bf16),
+            pltpu.VMEM((work * latent_count, width), bf16),
+            pltpu.VMEM((work * tokens, inner), bf16),
+            pltpu.VMEM((work * tokens, inner), bf16),
+            pltpu.VMEM((2 * inner, context_rows), bf16),
+        ],
+        compiler_params=pltpu.CompilerParams(vmem_limit_bytes=56 << 20),
+    )(full, alive, latents, queries, key_weight, value_weight, out_weight)
+
+
+DEPTH = 16
+CORES = 2
+
+
+def reduce_body(
+    n_dp,
+    n_mp,
+    partial_ref,
+    grads_ref,
+    alive_ref,
+    latents_ref,
+    resampled_ref,
+    key_ref,
+    value_ref,
+    y_relay,
+    y_sum,
+    y_got,
+    core_got,
+    x_sum,
+    x_relay,
+    x_got,
+    z_send,
+    z_got,
+    last,
+    last_got,
+    y_sems,
+    core_sems,
+    x_sems,
+    z_sems,
+    last_sems,
+):
+    f32, bf16 = jnp.float32, jnp.bfloat16
+    work, latent_count, quarter = resampled_ref.shape
+    inner = key_ref.shape[1]
+    n_x = n_dp // (DEPTH * CORES)
+    me_d = lax.axis_index("dp")
+    me_m = lax.axis_index("mp")
+    me_core = lax.rem(me_d, CORES)
+    me_z = lax.rem(me_d // CORES, DEPTH)
+    me_x = me_d // (DEPTH * CORES)
+
+    def at(x, z, core):
+        return (x * DEPTH + z) * CORES + core
+
+    y_right, y_left = lax.rem(me_m + 1, n_mp), lax.rem(me_m + n_mp - 1, n_mp)
+    y_far = lax.rem(me_m + 2, n_mp)
+    x_right, x_left = lax.rem(me_x + 1, n_x), lax.rem(me_x + n_x - 1, n_x)
+    x_far = lax.rem(me_x + 2, n_x)
+    other = 1 - me_core
+    dp_right, dp_left = at(x_right, me_z, me_core), at(x_left, me_z, me_core)
+    dp_other = at(me_x, me_z, other)
+
+    def z_of(o):
+        return lax.rem(me_z + o, DEPTH)
+
+    barrier = pltpu.get_barrier_semaphore()
+    partners = [(me_d, y_right), (me_d, y_left)]
+    partners += [(d, me_m) for d in (dp_right, dp_left, dp_other)]
+    partners += [(at(me_x, z_of(o), me_core), me_m) for o in range(1, DEPTH)]
+    for d, m in partners:
+        pl.semaphore_signal(barrier, inc=1, device_id={"dp": d, "mp": m}, device_id_type=MESH)
+    pl.semaphore_wait(barrier, len(partners))
+
+    def remote(src, dst, sems, i, d, m):
+        return pltpu.make_async_remote_copy(
+            src_ref=src,
+            dst_ref=dst,
+            send_sem=sems.at[0, i],
+            recv_sem=sems.at[1, i],
+            device_id={"dp": d, "mp": m},
+            device_id_type=MESH,
+        )
+
+    half_w = work // 2
+    low, high = pl.ds(0, half_w), pl.ds(half_w, half_w)
+    half_r = inner // 2
+    top, bottom = pl.ds(0, half_r), pl.ds(half_r, half_r)
+    y_copies = [
+        remote(partial_ref.at[y_far, low], y_relay.at[0], y_sems, 0, me_d, y_right),
+        remote(partial_ref.at[y_far, high], y_relay.at[1], y_sems, 1, me_d, y_left),
+        remote(partial_ref.at[y_right, high], y_got.at[0, high], y_sems, 2, me_d, y_right),
+        remote(partial_ref.at[y_left, low], y_got.at[1, low], y_sems, 3, me_d, y_left),
+        remote(y_sum.at[0], y_got.at[0, low], y_sems, 4, me_d, y_right),
+        remote(y_sum.at[1], y_got.at[1, high], y_sems, 5, me_d, y_left),
+    ]
+    x_copies = [
+        remote(x_sum.at[x_far, top], x_relay.at[0], x_sems, 0, dp_right, me_m),
+        remote(x_sum.at[x_far, bottom], x_relay.at[1], x_sems, 1, dp_left, me_m),
+        remote(x_sum.at[x_right, bottom], x_got.at[0, bottom], x_sems, 2, dp_right, me_m),
+        remote(x_sum.at[x_left, top], x_got.at[1, top], x_sems, 3, dp_left, me_m),
+        remote(x_sum.at[x_right, top], x_got.at[0, top], x_sems, 4, dp_right, me_m),
+        remote(x_sum.at[x_left, bottom], x_got.at[1, bottom], x_sems, 5, dp_left, me_m),
+    ]
+    order = (x_far, x_right, x_left, me_x)
+    other_order = order
+    core_copies = [
+        remote(grads_ref.at[other, x], core_got.at[x], core_sems, i, dp_other, me_m)
+        for i, x in enumerate(other_order)
+    ]
+    for i in range(4):
+        core_copies[i].start()
+        y_copies[i].start()
+
+    def join_cores(i):
+        core_copies[i].wait_recv()
+        x = order[i]
+        x_sum[x] = (grads_ref[me_core, x].astype(f32) + core_got[x].astype(f32)).astype(bf16)
+
+    join_cores(0)
+    x_copies[0].start()
+    x_copies[1].start()
+    join_cores(1)
+    x_copies[2].start()
+    join_cores(2)
+    x_copies[3].start()
+
+    y_copies[0].wait_recv()
+    y_sum[0] = (partial_ref[y_right, low].astype(f32) + y_relay[0].astype(f32)).astype(bf16)
+    y_copies[4].start()
+    y_copies[1].wait_recv()
+    y_sum[1] = (partial_ref[y_left, high].astype(f32) + y_relay[1].astype(f32)).astype(bf16)
+    y_copies[5].start()
+
+    join_cores(3)
+    x_copies[0].wait_recv()
+    x_sum[x_right, top] = (x_sum[x_right, top].astype(f32) + x_relay[0].astype(f32)).astype(bf16)
+    x_copies[4].start()
+    x_copies[1].wait_recv()
+    x_sum[x_left, bottom] = (x_sum[x_left, bottom].astype(f32) + x_relay[1].astype(f32)).astype(
+        bf16
     )
-
-
-def layer_norm(rows_in):
-    average = jnp.mean(rows_in, axis=-1, keepdims=True)
-    centred = rows_in - average
-    spread = jnp.mean(centred * centred, axis=-1, keepdims=True)
-    return centred * lax.rsqrt(spread + norm_epsilon)
+    x_copies[5].start()
+    for i in range(2, 6):
+        x_copies[i].wait_recv()
+    total = x_sum[me_x].astype(f32) + x_got[0].astype(f32) + x_got[1].astype(f32)
+    rows = total.T
+    share = quarter // DEPTH
+    for z in range(DEPTH):
+        piece = rows[z * share : (z + 1) * share, :]
+        z_send[z] = jnp.concatenate([piece[:, :128], piece[:, 128:]], axis=0).astype(bf16)
+    z_copies = {
+        o: remote(
+            z_send.at[z_of(o)],
+            z_got.at[o - 1],
+            z_sems,
+            o - 1,
+            at(me_x, z_of(o), me_core),
+            me_m,
+        )
+        for o in range(1, DEPTH)
+    }
+    for o in sorted(range(1, DEPTH), key=lambda o: -min(o, DEPTH - o)):
+        z_copies[o].start()
+
+    for i in range(2, 6):
+        y_copies[i].wait_recv()
+    mine = latents_ref[:, pl.ds(pl.multiple_of(me_m * quarter, 128), quarter)].astype(f32)
+    for w in range(work):
+        alive = jnp.concatenate([alive_ref[w : w + 1, :]] * (quarter // 128), axis=1)
+        summed = partial_ref[me_m, w].astype(f32) + y_got[0, w].astype(f32)
+        summed = summed + y_got[1, w].astype(f32)
+        resampled_ref[w] = ((mine + summed) * alive).astype(bf16)
+
+    total = z_send[me_z].astype(f32)
+    for o in sorted(range(1, DEPTH), key=lambda o: min(o, DEPTH - o)):
+        z_copies[o].wait_recv()
+        total = total + z_got[o - 1].astype(f32)
+    last[...] = total
+    last_copy = remote(last, last_got, last_sems, 0, dp_other, me_m)
+    last_copy.start()
+    last_copy.wait_recv()
+    first_core = me_core == 0
+    ours, theirs = last[...], last_got[...]
+    for out, block in (
+        (key_ref, jnp.where(first_core, ours, theirs)),
+        (value_ref, jnp.where(first_core, theirs, ours)),
+    ):
+        each = share // CORES
+        for half in range(2):
+            piece = block[half * share : (half + 1) * share, :]
+            out[:, half * 128 : (half + 1) * 128] = jnp.where(
+                first_core, piece[:each, :], piece[each:, :]
+            )
+    for copy in y_copies + x_copies + core_copies + list(z_copies.values()) + [last_copy]:
+        copy.wait_send()
+
+
+def reduce(n_dp, n_mp, partial, grads, alive, latents):
+    work, latent_count, quarter = partial.shape[1:]
+    inner = grads.shape[2]
+    n_x = n_dp // (DEPTH * CORES)
+    f32, bf16 = jnp.float32, jnp.bfloat16
+    vmem = pl.BlockSpec(memory_space=pltpu.VMEM)
+    dma = pltpu.SemaphoreType.DMA
+    share = quarter // DEPTH
+    half = (2, work // 2, latent_count, quarter)
+    return pl.pallas_call(
+        functools.partial(reduce_body, n_dp, n_mp),
+        name="reduce",
+        out_shape=(
+            jax.ShapeDtypeStruct((work, latent_count, quarter), bf16),
+            jax.ShapeDtypeStruct((share // CORES, inner), f32),
+            jax.ShapeDtypeStruct((share // CORES, inner), f32),
+        ),
+        in_specs=[vmem] * 4,
+        out_specs=(vmem,) * 3,
+        scratch_shapes=[
+            pltpu.VMEM(half, bf16),
+            pltpu.VMEM(half, bf16),
+            pltpu.VMEM((2, work, latent_count, quarter), bf16),
+            pltpu.VMEM((n_x, inner, quarter), bf16),
+            pltpu.VMEM((n_x, inner, quarter), bf16),
+            pltpu.VMEM((2, inner // 2, quarter), bf16),
+            pltpu.VMEM((2, inner, quarter), bf16),
+            pltpu.VMEM((DEPTH, 2 * share, 128), bf16),
+            pltpu.VMEM((DEPTH - 1, 2 * share, 128), bf16),
+            pltpu.VMEM((2 * share, 128), f32),
+            pltpu.VMEM((2 * share, 128), f32),
+            dma((2, 6)),
+            dma((2, n_x)),
+            dma((2, 6)),
+            dma((2, DEPTH - 1)),
+            dma((2, 1)),
+        ],
+        compiler_params=pltpu.CompilerParams(
+            collective_id=1, has_side_effects=True, vmem_limit_bytes=48 << 20
+        ),
+    )(partial, grads, alive, latents)
 
 
 def local(
@@ -286,126 +669,12 @@
     out_weight,
     cotangent,
 ):
-    image_tokens = media.shape[1]
-    quarter = media.shape[2]
-    work_slots = cotangent.shape[0]
-    latent_count = cotangent.shape[1]
-    model_width = latents.shape[1]
-    inner_dev = queries.shape[1]
-    head_count = inner_dev // HEAD
-    context_rows = image_tokens + latent_count
-    n_mp = lax.axis_size("mp")
-    full, alive = gather(lax.axis_size("dp"), n_mp, plan, doc_images, media, time_table, cotangent)
-    alive_slot = alive[:work_slots, 0]
-    whole = full.transpose(2, 1, 3, 0, 4).reshape(work_slots, image_tokens + latent_count, model_width)
-    full_media, cot_full = whole[:, :image_tokens], whole[:, image_tokens:]
-    normed = layer_norm(full_media.astype(jnp.float32)).astype(jnp.bfloat16)
-    normed_flat = normed.reshape(work_slots * image_tokens, model_width)
-    latent_norm = layer_norm(latents.astype(jnp.float32)).astype(jnp.bfloat16)
-    media_keys = (
-        jnp.dot(normed_flat, key_weight, preferred_element_type=jnp.float32)
-        .astype(jnp.bfloat16)
-        .reshape(work_slots, image_tokens, inner_dev)
+    n_dp, n_mp = lax.axis_size("dp"), lax.axis_size("mp")
+    full, alive = gather(n_dp, n_mp, plan, doc_images, media, time_table, cotangent)
+    partial_out, grads = attend(
+        full, alive, latents, queries, key_weight, value_weight, out_weight
     )
-    media_values = (
-        jnp.dot(normed_flat, value_weight, preferred_element_type=jnp.float32)
-        .astype(jnp.bfloat16)
-        .reshape(work_slots, image_tokens, inner_dev)
-    )
-    latent_keys = jnp.dot(latent_norm, key_weight, preferred_element_type=jnp.float32).astype(
-        jnp.bfloat16
-    )
-    latent_values = jnp.dot(latent_norm, value_weight, preferred_element_type=jnp.float32).astype(
-        jnp.bfloat16
-    )
-    key_rows = jnp.concatenate(
-        [media_keys, jnp.broadcast_to(latent_keys[None], (work_slots, latent_count, inner_dev))], 1
-    )
-    value_rows = jnp.concatenate(
-        [
-            media_values,
-            jnp.broadcast_to(latent_values[None], (work_slots, latent_count, inner_dev)),
-        ],
-        1,
-    )
-    key_heads = key_rows.reshape(work_slots, context_rows, head_count, HEAD)
-    value_heads = value_rows.reshape(work_slots, context_rows, head_count, HEAD)
-    query_heads = queries.reshape(latent_count, head_count, HEAD)
-    scores = (
-        jnp.einsum("qhe,wkhe->whqk", query_heads, key_heads, preferred_element_type=jnp.float32)
-        * 0.125
-    )
-    attention = jax.nn.softmax(scores, axis=-1)
-    attention_b = attention.astype(jnp.bfloat16)
-    attended = jnp.einsum(
-        "whqk,wkhe->wqhe", attention_b, value_heads, preferred_element_type=jnp.float32
-    ).astype(jnp.bfloat16)
-    attended_flat = attended.reshape(work_slots * latent_count, inner_dev)
-    partial_out = jnp.dot(attended_flat, out_weight, preferred_element_type=jnp.float32).reshape(
-        work_slots, latent_count, model_width
-    )
-    summed_heads = summed_on_arrival(partial_out.astype(jnp.bfloat16), "mp", 2)
-    latent_part = lax.dynamic_slice_in_dim(
-        latents, lax.axis_index("mp") * quarter, quarter, 1
-    ).astype(jnp.float32)
-    resampled = ((latent_part[None] + summed_heads) * alive_slot[:, None, None]).astype(
-        jnp.bfloat16
-    )
-    cot_live = cot_full * alive_slot.astype(jnp.bfloat16)[:, None, None]
-    grad_attended = lax.dot_general(
-        cot_live.reshape(work_slots * latent_count, model_width),
-        out_weight,
-        (((1,), (1,)), ((), ())),
-        preferred_element_type=jnp.float32,
-    ).astype(jnp.bfloat16)
-    grad_heads = grad_attended.reshape(work_slots, latent_count, head_count, HEAD)
-    grad_weights = jnp.einsum(
-        "wqhe,wkhe->whqk", grad_heads, value_heads, preferred_element_type=jnp.float32
-    )
-    row_dot = jnp.sum(attention * grad_weights, axis=-1, keepdims=True)
-    grad_scores = attention * (grad_weights - row_dot)
-    grad_keys = (
-        (
-            jnp.einsum(
-                "whqk,qhe->wkhe",
-                grad_scores,
-                query_heads.astype(jnp.float32),
-                precision=lax.Precision.HIGHEST,
-            )
-            * 0.125
-        )
-        .astype(jnp.bfloat16)
-        .reshape(work_slots, context_rows, inner_dev)
-    )
-    grad_values = (
-        jnp.einsum("whqk,wqhe->wkhe", attention_b, grad_heads, preferred_element_type=jnp.float32)
-        .astype(jnp.bfloat16)
-        .reshape(work_slots, context_rows, inner_dev)
-    )
-    media_grads = jnp.concatenate(
-        [grad_keys[:, :image_tokens], grad_values[:, :image_tokens]], 2
-    ).reshape(work_slots * image_tokens, 2 * inner_dev)
-    latent_grads = jnp.concatenate(
-        [
-            jnp.sum(grad_keys[:, image_tokens:].astype(jnp.float32), axis=0),
-            jnp.sum(grad_values[:, image_tokens:].astype(jnp.float32), axis=0),
-        ],
-        1,
-    )
-    latent_norm32 = latent_norm.astype(jnp.float32)
-    inverse_slots = 1.0 / (lax.axis_size("dp") * work_slots)
-    media_part = lax.dot_general(
-        normed_flat, media_grads, (((0,), (0,)), ((), ())), preferred_element_type=jnp.float32
-    )
-    latent_term = lax.dot_general(
-        latent_norm32,
-        latent_grads,
-        (((0,), (0,)), ((), ())),
-        precision=lax.Precision.HIGHEST,
-        preferred_element_type=jnp.float32,
-    )
-    shares = summed_on_arrival(((media_part + latent_term) * inverse_slots).astype(jnp.bfloat16), "dp", 0)
-    return (resampled, shares[:, :inner_dev], shares[:, inner_dev:])
+    return reduce(n_dp, n_mp, partial_out, grads, alive, latents)
 
 
 def solution(mesh):

time: 228 us -> 115 us (0.50)
  waiting for transfers between devices: 97.1 us -> 0 us
  Pallas kernels: 52.6 us -> 103 us
  matrix products: 21.5 us -> 0 us
  starting transfers between devices: 15.7 us -> 0 us
  local copies, waits for them, and re-layouts: 26.4 us -> 11.2 us
  other arithmetic: 12.5 us -> 0 us
    all_to_all x2 -> x0, waiting for transfers between devices: 97.1 us -> none  [summed_on_arrival(): pieces = lax.all_to_all(in_blocks(x, dim, size), axis, 0, 0, tiled=True)]
    pallas_call x0 -> x2, Pallas kernels: none -> 50.2 us  [the longest x1 30.8 us: reduce(): pl.pallas_call(functools.partial(reduce_body, n_dp, n_mp), name='reduce',...]
    dot_general x12 -> x0, matrix products: 19.6 us -> none  [the longest x1 4.01 us: local(): lax.dot_general(normed_flat, media_grads, (((0,), (0,)), ((), ())), prefe...]
    all_to_all x2 -> x0, starting transfers between devices: 15.7 us -> none  [summed_on_arrival(): pieces = lax.all_to_all(in_blocks(x, dim, size), axis, 0, 0, tiled=True)]
    reshape x6 -> x0, local copies, waits for them, and re-layouts: 10.2 us -> none  [the longest x1 7.32 us: local(): full.transpose(2, 1, 3, 0, 4)]
    reduce_sum x7 -> x0, other arithmetic: 9.53 us -> none  [the longest x2 4.01 us: layer_norm(): spread = jnp.mean(centred * centred, axis=-1, keepdims=True)]
    transpose x1 -> x0, local copies, waits for them, and re-layouts: 5.3 us -> none  [local(): full.transpose(2, 1, 3, 0, 4)]
    unnamed x30 -> x25, local copies, waits for them, and re-layouts: 6.05 us -> 11.2 us
  transfers between devices with their start and end apart: 2 -> 0, of which waited for: 1 -> 0; matrix products, arithmetic and copies ran while one was open for 9% -> 0% of each run, Pallas kernels for 0% -> 0%
where the time goes in v2:
time: 115 us
  Pallas kernels  103 us (90%)
  local copies, waits for them, and re-layouts  11.2 us (10%)
    pallas_call x1, Pallas kernels, gather(): pl.pallas_call(functools.partial(gather_body, n_dp, n_mp), name='route_an...  52.6 us
    pallas_call x1, Pallas kernels, reduce(): pl.pallas_call(functools.partial(reduce_body, n_dp, n_mp), name='reduce',...  30.8 us
    pallas_call x1, Pallas kernels, attend(): pl.pallas_call(attend_body, name='attend', out_shape=(jax.ShapeDtypeStruc...  19.4 us
    unnamed x25, local copies, waits for them, and re-layouts  11.2 us

profile of v2, /device:TPU:1, one launch (start us, length us, event | category | flops | bytes accessed | tf_op | source)
XLA Modules:
  0.0 114.7 jit_solution(480019790435107681)
XLA Ops:
  0.6 0.0 copy-start.2
  0.6 1.4 %copy-done.2 = bf16[8,256,384]{2,1,0:T(8,128)(2,1)S(1)} copy-done((bf16[8,256,384]{2,1,0:T(8,128)(2,1)S(1)}, bf16[8,256,384]{2,1,0:T(8,128)(2,1)}, u32[]{:S(2)}) %copy-start.2) | copy-done | bytes 1572888
  2.0 0.0 copy-start.5
  2.0 0.9 copy-done.5
  3.0 0.0 copy-start.8
  3.0 0.7 copy-done.8
  3.7 0.0 copy-start.9
  3.7 0.7 copy-done.9
  4.3 0.0 copy-start.10
  4.3 0.7 copy-done.10
  5.0 52.6 %route_and_gather.1 = (bf16[4,5,4,64,384]{4,3,2,1,0:T(8,128)(2,1)S(1)}, f32[8,128]{1,0:T(8,128)S(1)}) custom-call(s32[1,8]{1,0:T(1,128)S(1)} %copy-done.9, s32[2]{0:T(128)S(1)} %copy-done.10, bf16[8,256,384]{2,1,0:T(8,128)(2,1)S(1)} %copy-done.2, bf16[8,384]{1,0:T(8,128)(2,1)S(1)} %copy-done.8, bf16[4,64,384]{2,1,0:T(8,128)(2,1)S(1)} %copy-done.5), custom_call_target="tpu_custom_call" | custom-call | tf_op jit(solution)/shard_map/route_and_gather/pallas_call | solution.py:223
  57.6 0.0 copy-start
  57.6 1.8 %copy-done = bf16[4,5,4,64,384]{4,3,2,1,0:T(8,128)(2,1)} copy-done((bf16[4,5,4,64,384]{4,3,2,1,0:T(8,128)(2,1)}, bf16[4,5,4,64,384]{4,3,2,1,0:T(8,128)(2,1)S(1)}, u32[]{:S(2)}) %copy-start) | copy-done | bytes 3932184
  59.5 0.0 copy-start.6
  59.5 0.6 copy-done.6
  60.1 0.0 copy-start.3
  60.1 0.0 copy-start.7
  60.1 19.4 %attend.1 = (bf16[4,4,64,384]{3,2,1,0:T(8,128)(2,1)}, bf16[2,4,256,384]{3,2,1,0:T(8,128)(2,1)}) custom-call(bf16[4,5,4,64,384]{4,3,2,1,0:T(8,128)(2,1)} %copy-done, f32[8,128]{1,0:T(8,128)} %copy-done.6, bf16[64,1536]{1,0:T(8,128)(2,1)} %latents_ref.3, bf16[64,256]{1,0:T(8,128)(2,1)} %queries_ref.1, bf16[1536,256]{1,0:T(8,128)(2,1)} %key_weight_ref.1, ...), custom_call_target="tpu_custom_call" | custom-call | tf_op jit(solution)/shard_map/attend/pallas_call | solution.py:410
  79.4 0.0 copy-done.3
  79.5 0.0 copy-done.7
  79.5 0.0 copy-start.1
  79.5 1.4 %copy-done.1 = bf16[2,4,256,384]{3,2,1,0:T(8,128)(2,1)S(1)} copy-done((bf16[2,4,256,384]{3,2,1,0:T(8,128)(2,1)S(1)}, bf16[2,4,256,384]{3,2,1,0:T(8,128)(2,1)}, u32[]{:S(2)}) %copy-start.1) | copy-done | bytes 1572888
  80.9 0.0 copy-start.4
  80.9 1.1 copy-done.4
  82.0 30.8 %reduce.1 = (bf16[4,64,384]{2,1,0:T(8,128)(2,1)S(1)}, f32[12,256]{1,0:T(8,128)S(1)}, f32[12,256]{1,0:T(8,128)S(1)}) custom-call(bf16[4,4,64,384]{3,2,1,0:T(8,128)(2,1)S(1)} %copy-done.4, bf16[2,4,256,384]{3,2,1,0:T(8,128)(2,1)S(1)} %copy-done.1, f32[8,128]{1,0:T(8,128)S(1)} %copy-done.7, bf16[64,1536]{1,0:T(8,128)(2,1)S(1)} %copy-done.3), custom_call_target="tpu_custom_call" | custom-call | tf_op jit(solution)/shard_map/reduce/pallas_call | solution.py:626
  112.8 0.7 copy.16
  113.5 0.6 copy.17
  114.1 0.6 copy.18
Async XLA Ops:
  0.6 1.4 %copy-start.2 = (bf16[8,256,384]{2,1,0:T(8,128)(2,1)S(1)}, bf16[8,256,384]{2,1,0:T(8,128)(2,1)}, u32[]{:S(2)}) copy-start(bf16[8,256,384]{2,1,0:T(8,128)(2,1)} %media_ref.1) | copy-start | bytes 4718596
  2.0 0.9 copy-start.5
  3.0 0.7 copy-start.8
  3.7 0.7 copy-start.9
  4.3 0.7 copy-start.10
  57.6 1.9 %copy-start = (bf16[4,5,4,64,384]{4,3,2,1,0:T(8,128)(2,1)}, bf16[4,5,4,64,384]{4,3,2,1,0:T(8,128)(2,1)S(1)}, u32[]{:S(2)}) copy-start(bf16[4,5,4,64,384]{4,3,2,1,0:T(8,128)(2,1)S(1)} %get-tuple-element.7.full_ref) | copy-start | bytes 11796484
  59.5 0.6 copy-start.6
  60.1 19.4 %copy-start.3 = (bf16[64,1536]{1,0:T(8,128)(2,1)S(1)}, bf16[64,1536]{1,0:T(8,128)(2,1)}, u32[]{:S(2)}) copy-start(bf16[64,1536]{1,0:T(8,128)(2,1)} %latents_ref.3) | copy-start | bytes 589828
  60.1 19.4 %copy-start.7 = (f32[8,128]{1,0:T(8,128)S(1)}, f32[8,128]{1,0:T(8,128)}, u32[]{:S(2)}) copy-start(f32[8,128]{1,0:T(8,128)} %copy-done.6) | copy-start | bytes 12292
  79.5 1.4 %copy-start.1 = (bf16[2,4,256,384]{3,2,1,0:T(8,128)(2,1)S(1)}, bf16[2,4,256,384]{3,2,1,0:T(8,128)(2,1)}, u32[]{:S(2)}) copy-start(bf16[2,4,256,384]{3,2,1,0:T(8,128)(2,1)} %get-tuple-element.10.grads_ref) | copy-start | bytes 4718596
  80.9 1.1 copy-start.4

commit v3 on v1

v3 whole, which is shorter than its diff:
```python
import functools

import jax
import jax.numpy as jnp
from jax import lax
from jax.experimental import pallas as pl
from jax.experimental.pallas import tpu as pltpu
from jax.sharding import PartitionSpec as P

HEAD = 64
MESH = pl.DeviceIdType.MESH
CHUNKS = 4
REACH = 4

DEPTH = 16
CORES = 2

norm_epsilon = 1e-05


def plan_scalars(plan_ref, docs_ref, slots, work):
    far_slot = [jnp.int32(0)] * (REACH + 1)
    far_work = [jnp.int32(-1)] * (REACH + 1)
    own_slot = [jnp.int32(0)] * work
    own_live = [jnp.int32(0)] * work
    for s in range(slots):
        code = plan_ref[0, s]
        for k in range(1, REACH + 1):
            inside = (code >= k * work) & (code < (k + 1) * work)
            far_slot[k] = jnp.where(inside, s, far_slot[k])
            far_work[k] = jnp.where(inside, code - k * work, far_work[k])
        for w in range(work):
            own_slot[w] = jnp.where(code == w, s, own_slot[w])
            own_live[w] = jnp.where(code == w, 1, own_live[w])
    first = docs_ref[0]

    def position(s):
        return s - jnp.where(s >= first, first, 0)

    return far_slot, far_work, own_slot, own_live, position


def normalise(parts, width):
    parts = [p.astype(jnp.float32) for p in parts]
    average = sum(jnp.sum(p, axis=-1, keepdims=True) for p in parts) * (1.0 / width)
    parts = [p - average for p in parts]
    spread = sum(jnp.sum(p * p, axis=-1, keepdims=True) for p in parts) * (1.0 / width)
    scale = lax.rsqrt(spread + norm_epsilon)
    return [(p * scale).astype(jnp.bfloat16) for p in parts]


def dot(a, b, dims=(1, 0)):
    return lax.dot_general(
        a, b, (((dims[0],), (dims[1],)), ((), ())), preferred_element_type=jnp.float32
    )


def body(
    n_dp,
    n_mp,
    plan_hbm,
    docs_hbm,
    time_hbm,
    media_hbm,
    cot_hbm,
    queries_hbm,
    latents_hbm,
    key_weight_hbm,
    value_weight_hbm,
    out_weight_hbm,
    resampled_ref,
    key_ref,
    value_ref,
    plan_ref,
    docs_ref,
    time_ref,
    media_ref,
    queries_ref,
    latents_ref,
    key_weight_ref,
    value_weight_ref,
    out_weight_ref,
    send_buf,
    head_buf,
    got_buf,
    got_head,
    full,
    context,
    cot_live,
    keys,
    values,
    grad_attended,
    grads,
    partial,
    y_relay,
    y_sum,
    y_got,
    core_send,
    core_got,
    x_own,
    x_sum,
    x_relay,
    x_got,
    z_send,
    z_got,
    last,
    last_got,
    local_sems,
    far_sems,
    head_sems,
    ring_sems,
    y_sems,
    core_sems,
    x_sems,
    z_sems,
    last_sems,
):
    f32, bf16 = jnp.float32, jnp.bfloat16
    slots, tokens, quarter = media_hbm.shape
    work, latent_count = cot_hbm.shape[:2]
    width = latents_hbm.shape[1]
    inner = queries_hbm.shape[1]
    heads = inner // HEAD
    rows = tokens // CHUNKS
    half_w = work // 2
    n_x = n_dp // (DEPTH * CORES)
    me_d = lax.axis_index("dp")
    me_m = lax.axis_index("mp")
    me_core = lax.rem(me_d, CORES)
    me_z = lax.rem(me_d // CORES, DEPTH)
    me_x = me_d // (DEPTH * CORES)

    def at(x, z, core):
        return (x * DEPTH + z) * CORES + core

    def far(k):
        return lax.rem(me_d + (k + n_dp), n_dp)

    def z_of(o):
        return lax.rem(me_z + o, DEPTH)

    y_right, y_left = lax.rem(me_m + 1, n_mp), lax.rem(me_m + n_mp - 1, n_mp)
    y_far = lax.rem(me_m + 2, n_mp)
    x_right, x_left = lax.rem(me_x + 1, n_x), lax.rem(me_x + n_x - 1, n_x)
    x_far = lax.rem(me_x + 2, n_x)
    other = 1 - me_core
    dp_right, dp_left = at(x_right, me_z, me_core), at(x_left, me_z, me_core)
    dp_other = at(me_x, me_z, other)

    arguments = [
        (plan_hbm, plan_ref),
        (docs_hbm, docs_ref),
        (time_hbm, time_ref),
    ]
    arguments += [
        (media_hbm, media_ref),
        (cot_hbm, full.at[me_m, CHUNKS]),
        (latents_hbm, latents_ref),
        (key_weight_hbm, key_weight_ref),
        (value_weight_hbm, value_weight_ref),
        (queries_hbm, queries_ref),
        (out_weight_hbm, out_weight_ref),
    ]
    loads = [
        pltpu.make_async_copy(src, dst, local_sems.at[i]) for i, (src, dst) in enumerate(arguments)
    ]
    for load in loads:
        load.start()

    barrier = pltpu.get_barrier_semaphore()
    partners = [(at(me_x, z_of(o), me_core), me_m) for o in range(DEPTH - 1, 0, -1)]
    for k in range(1, REACH + 1):
        partners += [(far(k), me_m), (far(-k), me_m)]
    partners += [(d, me_m) for d in (dp_right, dp_left, dp_other)]
    partners += [(me_d, y_right), (me_d, y_left)]
    for d, m in partners:
        pl.semaphore_signal(barrier, inc=1, device_id={"dp": d, "mp": m}, device_id_type=MESH)

    for load in loads[:4]:
        load.wait()
    far_slot, far_work, own_slot, own_live, position = plan_scalars(
        plan_ref, docs_ref, slots, work
    )
    times = time_ref[...].astype(f32)
    time_rows = lax.broadcasted_iota(jnp.int32, times.shape, 0)

    def time_of(s):
        return jnp.sum(jnp.where(time_rows == position(s), times, 0.0), axis=0, keepdims=True)

    mark_rows = lax.broadcasted_iota(jnp.int32, head_buf.shape[1:], 0)
    far_rows = [None]
    for k in range(1, REACH + 1):
        head_buf[k - 1] = jnp.where(mark_rows == far_work[k], 1.0, 0.0).astype(bf16)
        far_rows.append(time_of(far_slot[k]))
    own_rows = [time_of(own_slot[w]) for w in range(work)]
    for c in range(CHUNKS):
        for k in range(1, REACH + 1):
            block = media_ref[far_slot[k], c * rows : (c + 1) * rows, :].astype(f32)
            send_buf[c, k - 1] = (block + far_rows[k]).astype(bf16)

    pl.semaphore_wait(barrier, len(partners))

    def remote(src, dst, sems, i, d, m):
        return pltpu.make_async_remote_copy(
            src_ref=src,
            dst_ref=dst,
            send_sem=sems.at[0, i],
            recv_sem=sems.at[1, i],
            device_id={"dp": d, "mp": m},
            device_id_type=MESH,
        )

    def own_sends(c, src):
        return [
            remote(src, full.at[me_m, c], ring_sems, 4 * c, me_d, y_right),
            remote(src, full.at[me_m, c], ring_sems, 4 * c + 1, me_d, y_left),
        ]

    def own_arrivals(c):
        return [
            remote(full.at[y_left, c], full.at[y_left, c], ring_sems, 4 * c, me_d, y_right),
            remote(full.at[y_right, c], full.at[y_right, c], ring_sems, 4 * c + 1, me_d, y_left),
        ]

    low, high = pl.ds(0, half_w), pl.ds(half_w, half_w)

    def forwards(c):
        first, second = full.at[y_left, c, low], full.at[y_right, c, high]
        return [
            remote(first, first, ring_sems, 4 * c + 2, me_d, y_right),
            remote(second, second, ring_sems, 4 * c + 3, me_d, y_left),
        ]

    def forward_arrivals(c):
        first, second = full.at[y_far, c, low], full.at[y_far, c, high]
        return [
            remote(first, first, ring_sems, 4 * c + 2, me_d, y_right),
            remote(second, second, ring_sems, 4 * c + 3, me_d, y_left),
        ]

    def far_copy(c, k):
        i = c * REACH + k - 1
        return remote(send_buf.at[c, k - 1], got_buf.at[c, k - 1], far_sems, i, far(k), me_m)

    def head_copy(k):
        return remote(head_buf.at[k - 1], got_head.at[k - 1], head_sems, k - 1, far(k), me_m)

    started = own_sends(CHUNKS, cot_hbm)
    for k in range(REACH, 0, -1):
        started.append(head_copy(k))
    for c in range(CHUNKS):
        for k in range(REACH, 0, -1):
            started.append(far_copy(c, k))
    for copy in started:
        copy.start()

    first_weight = 5
    for load in loads[first_weight - 1 : first_weight + 4]:
        load.wait()
    latent_norm = normalise([latents_ref[...]], width)[0]
    for w in range(work):
        where = work * tokens + w * latent_count
        context[where : where + latent_count, :] = latent_norm
    latent_keys = dot(latent_norm, key_weight_ref[...]).astype(bf16)
    latent_values = dot(latent_norm, value_weight_ref[...]).astype(bf16)
    row_head = lax.broadcasted_iota(jnp.int32, (heads * latent_count, inner), 0) // latent_count
    col_head = lax.broadcasted_iota(jnp.int32, (heads * latent_count, inner), 1) // HEAD
    same_head = row_head == col_head

    def spread_heads(x):
        return jnp.where(same_head, jnp.concatenate([x.astype(f32)] * heads, axis=0), 0.0)

    wide_queries32 = spread_heads(queries_ref[...])
    wide_queries = wide_queries32.astype(bf16)
    wide_queries_t = wide_queries32.T.astype(bf16)
    latent_scores = dot(latent_keys, wide_queries, (1, 1)) * 0.125
    loads[first_weight + 4].wait()

    for k in range(1, REACH + 1):
        head_copy(k).wait_recv()
    marks = [got_head[k].astype(f32) for k in range(REACH)]
    lives = [jnp.where(own_live[w] == 1, 1.0, 0.0) for w in range(work)]
    alive = [sum(marks[k][w : w + 1, :] for k in range(REACH)) + lives[w] for w in range(work)]

    def place(c):
        for k in range(1, REACH + 1):
            far_copy(c, k).wait_recv()
        for w in range(work):
            block = media_ref[own_slot[w], c * rows : (c + 1) * rows, :].astype(f32)
            block = (block + own_rows[w]) * lives[w]
            for k in range(REACH):
                block = block + marks[k][w : w + 1, :] * got_buf[c, k].astype(f32)
            full[me_m, c, w] = block.astype(bf16)
        return own_sends(c, full.at[me_m, c])

    sub = min(32, rows)

    def project(c):
        def norm_rows(i, carry):
            w, r = i // (rows // sub), i % (rows // sub)
            r = pl.multiple_of(r * sub, sub)
            pieces = normalise([full[m, c, w, pl.ds(r, sub), :] for m in range(n_mp)], width)
            where = pl.multiple_of(w * tokens + c * rows + r, sub)
            for m in range(n_mp):
                context[pl.ds(where, sub), m * quarter : (m + 1) * quarter] = pieces[m]
            return carry

        lax.fori_loop(0, work * (rows // sub), norm_rows, 0)
        places = [slice(w * tokens + c * rows, w * tokens + (c + 1) * rows) for w in range(work)]
        normed = jnp.concatenate([context[p, :] for p in places], axis=0)
        for out, weight in ((keys, key_weight_ref), (values, value_weight_ref)):
            product = dot(normed, weight[...]).astype(bf16)
            for w, p in enumerate(places):
                out[p, :] = product[w * rows : (w + 1) * rows, :]

    def pull_back():
        for w in range(work):
            for m in range(n_mp):
                cot_live[
                    w * latent_count : (w + 1) * latent_count, m * quarter : (m + 1) * quarter
                ] = (full[m, CHUNKS, w].astype(f32) * alive[w]).astype(bf16)
        grad_attended[...] = dot(cot_live[...], out_weight_ref[...], (1, 1)).astype(bf16)

    def finish(c):
        for copy in forward_arrivals(c):
            copy.wait_recv()
        if c == CHUNKS:
            pull_back()
        else:
            project(c)

    order = [CHUNKS] + list(range(CHUNKS))
    for i, c in enumerate(order):
        if i < CHUNKS:
            copies = place(i)
            for copy in copies:
                copy.start()
            started += copies
        for copy in own_arrivals(c):
            copy.wait_recv()
        copies = forwards(c)
        for copy in copies:
            copy.start()
        started += copies
        if i > 0:
            finish(order[i - 1])
    finish(order[-1])

    half_r = inner // 2
    top, bottom = pl.ds(0, half_r), pl.ds(half_r, half_r)
    y_copies = [
        remote(partial.at[y_far, low], y_relay.at[0], y_sems, 0, me_d, y_right),
        remote(partial.at[y_far, high], y_relay.at[1], y_sems, 1, me_d, y_left),
        remote(partial.at[y_right, high], y_got.at[0, high], y_sems, 2, me_d, y_right),
        remote(partial.at[y_left, low], y_got.at[1, low], y_sems, 3, me_d, y_left),
        remote(y_sum.at[0], y_got.at[0, low], y_sems, 4, me_d, y_right),
        remote(y_sum.at[1], y_got.at[1, high], y_sems, 5, me_d, y_left),
    ]
    for w in range(work):
        begin = w * tokens
        slot_keys = keys[begin : begin + tokens, :]
        slot_values = values[begin : begin + tokens, :]
        scores = dot(slot_keys, wide_queries, (1, 1)) * 0.125
        top_score = jnp.maximum(
            jnp.max(scores, axis=0, keepdims=True), jnp.max(latent_scores, axis=0, keepdims=True)
        )
        weight = jnp.exp(scores - top_score)
        latent_weight = jnp.exp(latent_scores - top_score)
        total = jnp.sum(weight, axis=0, keepdims=True) + jnp.sum(
            latent_weight, axis=0, keepdims=True
        )
        attention = weight / total
        latent_attention = latent_weight / total
        attention_b = attention.astype(bf16)
        latent_attention_b = latent_attention.astype(bf16)
        attended = dot(attention_b, slot_values, (0, 0)) + dot(
            latent_attention_b, latent_values, (0, 0)
        )
        attended = jnp.where(same_head, attended, 0.0)
        attended = sum(
            attended[h * latent_count : (h + 1) * latent_count, :] for h in range(heads)
        ).astype(bf16)
        part = dot(attended, out_weight_ref[...]).astype(bf16)
        for m in range(n_mp):
            partial[m, w] = part[:, m * quarter : (m + 1) * quarter]
        if w == half_w - 1:
            y_copies[0].start()
            y_copies[3].start()
        if w == work - 1:
            y_copies[1].start()
            y_copies[2].start()

        slot_grad = grad_attended[w * latent_count : (w + 1) * latent_count, :]
        wide_grad32 = spread_heads(slot_grad)
        wide_grad = wide_grad32.astype(bf16)
        wide_grad_t = wide_grad32.T.astype(bf16)
        slope = dot(slot_values, wide_grad, (1, 1))
        latent_slope = dot(latent_values, wide_grad, (1, 1))
        row_dot = jnp.sum(attention * slope, axis=0, keepdims=True) + jnp.sum(
            latent_attention * latent_slope, axis=0, keepdims=True
        )
        for where, count, att, att_b, slopes in (
            (begin, tokens, attention, attention_b, slope),
            (
                work * tokens + w * latent_count,
                latent_count,
                latent_attention,
                latent_attention_b,
                latent_slope,
            ),
        ):
            grad_scores = att * (slopes - row_dot)
            near = grad_scores.astype(bf16)
            rest = (grad_scores - near.astype(f32)).astype(bf16)
            grad_keys = (
                dot(wide_queries_t, near, (1, 1)) + dot(wide_queries_t, rest, (1, 1))
            ) * 0.125
            grads[0:inner, where : where + count] = grad_keys.astype(bf16)
            grads[inner : 2 * inner, where : where + count] = dot(
                wide_grad_t, att_b, (1, 1)
            ).astype(bf16)

    x_copies = [
        remote(x_sum.at[x_far, top], x_relay.at[0], x_sems, 0, dp_right, me_m),
        remote(x_sum.at[x_far, bottom], x_relay.at[1], x_sems, 1, dp_left, me_m),
        remote(x_sum.at[x_right, bottom], x_got.at[0, bottom], x_sems, 2, dp_right, me_m),
        remote(x_sum.at[x_left, top], x_got.at[1, top], x_sems, 3, dp_left, me_m),
        remote(x_sum.at[x_right, top], x_got.at[0, top], x_sems, 4, dp_right, me_m),
        remote(x_sum.at[x_left, bottom], x_got.at[1, bottom], x_sems, 5, dp_left, me_m),
    ]
    x_order = (x_far, x_right, x_left, me_x)
    core_copies = [
        remote(core_send.at[i], core_got.at[i], core_sems, i, dp_other, me_m) for i in range(n_x)
    ]
    inverse = 1.0 / (n_dp * work)

    def weight_grad(kind, x):
        left_side = grads[pl.ds(pl.multiple_of(kind * inner, inner), inner), :]
        right_side = context[:, pl.ds(pl.multiple_of(x * quarter, 128), quarter)]
        return dot(left_side, right_side) * inverse

    def join_cores(i):
        core_copies[i].wait_recv()
        x_sum[x_order[i]] = (x_own[i] + core_got[i].astype(f32)).astype(bf16)
        if i == 0:
            x_copies[0].start()
            x_copies[1].start()
        elif i < 3:
            x_copies[i + 1].start()

    for i, x in enumerate(x_order):
        core_send[i] = weight_grad(other, x).astype(bf16)
        core_copies[i].start()
        x_own[i] = weight_grad(me_core, x)
        if i > 0:
            join_cores(i - 1)

    y_copies[0].wait_recv()
    y_sum[0] = (partial[y_right, low].astype(f32) + y_relay[0].astype(f32)).astype(bf16)
    y_copies[4].start()
    y_copies[1].wait_recv()
    y_sum[1] = (partial[y_left, high].astype(f32) + y_relay[1].astype(f32)).astype(bf16)
    y_copies[5].start()
    join_cores(n_x - 1)
    x_copies[0].wait_recv()
    x_sum[x_right, top] = (x_sum[x_right, top].astype(f32) + x_relay[0].astype(f32)).astype(bf16)
    x_copies[4].start()
    x_copies[1].wait_recv()
    x_sum[x_left, bottom] = (x_sum[x_left, bottom].astype(f32) + x_relay[1].astype(f32)).astype(
        bf16
    )
    x_copies[5].start()
    for i in range(2, 6):
        x_copies[i].wait_recv()
    summed = (x_sum[me_x].astype(f32) + x_got[0].astype(f32) + x_got[1].astype(f32)).T
    share = quarter // DEPTH
    for z in range(DEPTH):
        piece = summed[z * share : (z + 1) * share, :]
        z_send[z] = jnp.concatenate([piece[:, :128], piece[:, 128:]], axis=0).astype(bf16)
    z_copies = {
        o: remote(
            z_send.at[z_of(o)],
            z_got.at[o - 1],
            z_sems,
            o - 1,
            at(me_x, z_of(o), me_core),
            me_m,
        )
        for o in range(1, DEPTH)
    }
    for o in sorted(range(1, DEPTH), key=lambda o: -min(o, DEPTH - o)):
        z_copies[o].start()

    for i in range(2, 6):
        y_copies[i].wait_recv()
    mine = latents_ref[:, pl.ds(pl.multiple_of(me_m * quarter, 128), quarter)].astype(f32)
    for w in range(work):
        heads_sum = partial[me_m, w].astype(f32) + y_got[0, w].astype(f32)
        heads_sum = heads_sum + y_got[1, w].astype(f32)
        resampled_ref[w] = ((mine + heads_sum) * alive[w]).astype(bf16)

    total = z_send[me_z].astype(f32)
    for o in sorted(range(1, DEPTH), key=lambda o: min(o, DEPTH - o)):
        z_copies[o].wait_recv()
        total = total + z_got[o - 1].astype(f32)
    last[...] = total
    last_copy = remote(last, last_got, last_sems, 0, dp_other, me_m)
    last_copy.start()
    last_copy.wait_recv()
    first_core = me_core == 0
    ours, theirs = last[...], last_got[...]
    each = share // CORES
    for out, block in (
        (key_ref, jnp.where(first_core, ours, theirs)),
        (value_ref, jnp.where(first_core, theirs, ours)),
    ):
        for half in range(2):
            piece = block[half * share : (half + 1) * share, :]
            out[:, half * 128 : (half + 1) * 128] = jnp.where(
                first_core, piece[:each, :], piece[each:, :]
            )
    for copy in started + y_copies + x_copies + core_copies + list(z_copies.values()) + [last_copy]:
        copy.wait_send()


def local(
    media,
    time_table,
    doc_images,
    plan,
    latents,
    queries,
    key_weight,
    value_weight,
    out_weight,
    cotangent,
):
    n_dp, n_mp = lax.axis_size("dp"), lax.axis_size("mp")
    slots, tokens, quarter = media.shape
    work, latent_count = cotangent.shape[:2]
    width = latents.shape[1]
    inner = queries.shape[1]
    rows = tokens // CHUNKS
    n_x = n_dp // (DEPTH * CORES)
    share = quarter // DEPTH
    context_rows = work * (tokens + latent_count)
    half = (2, work // 2, latent_count, quarter)
    f32, bf16 = jnp.float32, jnp.bfloat16
    vmem = pl.BlockSpec(memory_space=pltpu.VMEM)
    hbm = pl.BlockSpec(memory_space=pl.ANY)
    dma = pltpu.SemaphoreType.DMA

    def like(x):
        return pltpu.VMEM(x.shape, x.dtype)

    return pl.pallas_call(
        functools.partial(body, n_dp, n_mp),
        name="resample",
        out_shape=(
            jax.ShapeDtypeStruct((work, latent_count, quarter), bf16),
            jax.ShapeDtypeStruct((share // CORES, inner), f32),
            jax.ShapeDtypeStruct((share // CORES, inner), f32),
        ),
        in_specs=[hbm] * 10,
        out_specs=(vmem,) * 3,
        scratch_shapes=[
            pltpu.SMEM(plan.shape, jnp.int32),
            pltpu.SMEM(doc_images.shape, jnp.int32),
            like(time_table),
            like(media),
            like(queries),
            like(latents),
            like(key_weight),
            like(value_weight),
            like(out_weight),
            pltpu.VMEM((CHUNKS, REACH, rows, quarter), bf16),
            pltpu.VMEM((REACH, 16, quarter), bf16),
            pltpu.VMEM((CHUNKS, REACH, rows, quarter), bf16),
            pltpu.VMEM((REACH, 16, quarter), bf16),
            pltpu.VMEM((n_mp, CHUNKS + 1, work, rows, quarter), bf16),
            pltpu.VMEM((context_rows, width), bf16),
            pltpu.VMEM((work * latent_count, width), bf16),
            pltpu.VMEM((work * tokens, inner), bf16),
            pltpu.VMEM((work * tokens, inner), bf16),
            pltpu.VMEM((work * latent_count, inner), bf16),
            pltpu.VMEM((2 * inner, context_rows), bf16),
            pltpu.VMEM((n_mp, work, latent_count, quarter), bf16),
            pltpu.VMEM(half, bf16),
            pltpu.VMEM(half, bf16),
            pltpu.VMEM((2, work, latent_count, quarter), bf16),
            pltpu.VMEM((n_x, inner, quarter), bf16),
            pltpu.VMEM((n_x, inner, quarter), bf16),
            pltpu.VMEM((n_x, inner, quarter), f32),
            pltpu.VMEM((n_x, inner, quarter), bf16),
            pltpu.VMEM((2, inner // 2, quarter), bf16),
            pltpu.VMEM((2, inner, quarter), bf16),
            pltpu.VMEM((DEPTH, 2 * share, 128), bf16),
            pltpu.VMEM((DEPTH - 1, 2 * share, 128), bf16),
            pltpu.VMEM((2 * share, 128), f32),
            pltpu.VMEM((2 * share, 128), f32),
            dma((10,)),
            dma((2, CHUNKS * REACH)),
            dma((2, REACH)),
            dma((2, 4 * CHUNKS + 4)),
            dma((2, 6)),
            dma((2, n_x)),
            dma((2, 6)),
            dma((2, DEPTH - 1)),
            dma((2, 1)),
        ],
        compiler_params=pltpu.CompilerParams(
            collective_id=0, has_side_effects=True, vmem_limit_bytes=60 << 20
        ),
    )(
        plan,
        doc_images,
        time_table,
        media,
        cotangent,
        queries,
        latents,
        key_weight,
        value_weight,
        out_weight,
    )


def solution(mesh):
    return jax.shard_map(
        local,
        mesh=mesh,
        in_specs=(
            P("dp", None, "mp"),
            P(None, "mp"),
            P("dp"),
            P("dp", None),
            P(),
            P(None, "mp"),
            P(None, "mp"),
            P(None, "mp"),
            P("mp", None),
            P("dp", None, "mp"),
        ),
        out_specs=(P("dp", None, "mp"), P("dp", "mp"), P("dp", "mp")),
        check_vma=False,
    )
```

time: 228 us -> 94.7 us (0.42)
  waiting for transfers between devices: 97.1 us -> 0 us
  Pallas kernels: 52.6 us -> 89.5 us
  local copies, waits for them, and re-layouts: 26.4 us -> 4.27 us
  matrix products: 21.5 us -> 0 us
  starting transfers between devices: 15.7 us -> 0 us
  other arithmetic: 12.5 us -> 0 us
    all_to_all x2 -> x0, waiting for transfers between devices: 97.1 us -> none  [summed_on_arrival(): pieces = lax.all_to_all(in_blocks(x, dim, size), axis, 0, 0, tiled=True)]
    pallas_call x1, Pallas kernels: 52.6 us -> 89.5 us  [local(): pl.pallas_call(functools.partial(body, n_dp, n_mp), name='resample', out_...]
    dot_general x12 -> x0, matrix products: 19.6 us -> none  [the longest x1 4.01 us: local(): lax.dot_general(normed_flat, media_grads, (((0,), (0,)), ((), ())), prefe...]
    all_to_all x2 -> x0, starting transfers between devices: 15.7 us -> none  [summed_on_arrival(): pieces = lax.all_to_all(in_blocks(x, dim, size), axis, 0, 0, tiled=True)]
    reshape x6 -> x0, local copies, waits for them, and re-layouts: 10.2 us -> none  [the longest x1 7.32 us: local(): full.transpose(2, 1, 3, 0, 4)]
    reduce_sum x7 -> x0, other arithmetic: 9.53 us -> none  [the longest x2 4.01 us: layer_norm(): spread = jnp.mean(centred * centred, axis=-1, keepdims=True)]
    transpose x1 -> x0, local copies, waits for them, and re-layouts: 5.3 us -> none  [local(): full.transpose(2, 1, 3, 0, 4)]
    slice x4 -> x0, local copies, waits for them, and re-layouts: 2.43 us -> none  [the longest x1 0.85 us: local(): grad_values[:, :image_tokens]]
  transfers between devices with their start and end apart: 2 -> 0, of which waited for: 1 -> 0; matrix products, arithmetic and copies ran while one was open for 9% -> 0% of each run, Pallas kernels for 0% -> 0%
where the time goes in v3:
time: 94.7 us; the launch traced here: 94.4 us
  Pallas kernels  89.5 us (95%)
  local copies, waits for them, and re-layouts  4.27 us (5%)
    pallas_call x1, Pallas kernels, local(): pl.pallas_call(functools.partial(body, n_dp, n_mp), name='resample', out_...  89.5 us
    unnamed x3, local copies, waits for them, and re-layouts  4.27 us

profile of v3, /device:TPU:1, one launch (start us, length us, event | category | flops | bytes accessed | tf_op | source)
XLA Modules:
  0.0 94.4 jit_solution(3243091437997609551)
XLA Ops:
  0.6 89.5 %resample.1 = (bf16[4,64,384]{2,1,0:T(8,128)(2,1)}, f32[12,256]{1,0:T(8,128)}, f32[12,256]{1,0:T(8,128)}) custom-call(s32[1,8]{1,0:T(1,128)} %plan_hbm.1, s32[2]{0:T(128)} %docs_hbm.1, bf16[8,384]{1,0:T(8,128)(2,1)} %time_hbm.1, bf16[8,256,384]{2,1,0:T(8,128)(2,1)} %media_hbm.1, bf16[4,64,384]{2,1,0:T(8,128)(2,1)} %cot_hbm.1, bf16[64,256]{1,0:T(8,128)(2,1)} %queries_hbm.1, ...), custom_call_target="tpu_custom_call" | custom-call | tf_op jit(solution)/shard_map/resample/pallas_call | solution.py:556
  90.1 1.6 %copy.16 = bf16[4,64,384]{2,1,0:T(8,128)(2,1)} copy(bf16[4,64,384]{2,1,0:T(8,128)(2,1)} %get-tuple-element.6) | data formatting | bytes 393216
  91.8 1.3 %copy.17 = f32[12,256]{1,0:T(8,128)} copy(f32[12,256]{1,0:T(8,128)} %get-tuple-element.7) | data formatting | bytes 24576
  93.1 1.3 %copy.18 = f32[12,256]{1,0:T(8,128)} copy(f32[12,256]{1,0:T(8,128)} %get-tuple-element.8) | data formatting | bytes 24576

commit v4 on v3

--- a/solution.py
+++ b/solution.py
@@ -87,17 +87,20 @@
     full,
     context,
     cot_live,
-    keys,
     values,
-    grad_attended,
+    scores,
+    slopes,
+    latent_slopes,
+    wide_grads,
+    wide_grads_t,
+    attention,
     grads,
     partial,
     y_relay,
     y_sum,
     y_got,
-    core_send,
+    core_both,
     core_got,
-    x_own,
     x_sum,
     x_relay,
     x_got,
@@ -114,6 +117,7 @@
     x_sems,
     z_sems,
     last_sems,
+    known_sems,
 ):
     f32, bf16 = jnp.float32, jnp.bfloat16
     slots, tokens, quarter = media_hbm.shape
@@ -168,7 +172,7 @@
         load.start()
 
     barrier = pltpu.get_barrier_semaphore()
-    partners = [(at(me_x, z_of(o), me_core), me_m) for o in range(DEPTH - 1, 0, -1)]
+    partners = [(at(me_x, z_of(o), me_core), me_m) for o in (2, DEPTH - 2, 1, DEPTH - 1)]
     for k in range(1, REACH + 1):
         partners += [(far(k), me_m), (far(-k), me_m)]
     partners += [(d, me_m) for d in (dp_right, dp_left, dp_other)]
@@ -200,6 +204,17 @@
 
     pl.semaphore_wait(barrier, len(partners))
 
+    def greet(i, distance):
+        for o in (distance, DEPTH - distance):
+            pl.semaphore_signal(
+                known_sems.at[i],
+                inc=1,
+                device_id={"dp": at(me_x, z_of(o), me_core), "mp": me_m},
+                device_id_type=MESH,
+            )
+
+    greet(0, 2)
+
     def remote(src, dst, sems, i, d, m):
         return pltpu.make_async_remote_copy(
             src_ref=src,
@@ -260,7 +275,10 @@
     latent_norm = normalise([latents_ref[...]], width)[0]
     for w in range(work):
         where = work * tokens + w * latent_count
-        context[where : where + latent_count, :] = latent_norm
+        for m in range(n_mp):
+            context[m, where : where + latent_count, :] = latent_norm[
+                :, m * quarter : (m + 1) * quarter
+            ]
     latent_keys = dot(latent_norm, key_weight_ref[...]).astype(bf16)
     latent_values = dot(latent_norm, value_weight_ref[...]).astype(bf16)
     row_head = lax.broadcasted_iota(jnp.int32, (heads * latent_count, inner), 0) // latent_count
@@ -302,16 +320,26 @@
             pieces = normalise([full[m, c, w, pl.ds(r, sub), :] for m in range(n_mp)], width)
             where = pl.multiple_of(w * tokens + c * rows + r, sub)
             for m in range(n_mp):
-                context[pl.ds(where, sub), m * quarter : (m + 1) * quarter] = pieces[m]
+                context[m, pl.ds(where, sub), :] = pieces[m]
             return carry
 
         lax.fori_loop(0, work * (rows // sub), norm_rows, 0)
         places = [slice(w * tokens + c * rows, w * tokens + (c + 1) * rows) for w in range(work)]
-        normed = jnp.concatenate([context[p, :] for p in places], axis=0)
-        for out, weight in ((keys, key_weight_ref), (values, value_weight_ref)):
-            product = dot(normed, weight[...]).astype(bf16)
-            for w, p in enumerate(places):
-                out[p, :] = product[w * rows : (w + 1) * rows, :]
+        normed = [
+            jnp.concatenate([context[m, p, :] for p in places], axis=0) for m in range(n_mp)
+        ]
+
+        def product(weight):
+            return sum(
+                dot(normed[m], weight[m * quarter : (m + 1) * quarter, :]) for m in range(n_mp)
+            ).astype(bf16)
+
+        new_keys, new_values = product(key_weight_ref), product(value_weight_ref)
+        new_scores = dot(new_keys, wide_queries, (1, 1)) * 0.125
+        for w, p in enumerate(places):
+            values[p, :] = new_values[w * rows : (w + 1) * rows, :]
+            scores[p, :] = new_scores[w * rows : (w + 1) * rows, :]
+            slopes[p, :] = dot(new_values[w * rows : (w + 1) * rows, :], wide_grads[w], (1, 1))
 
     def pull_back():
         for w in range(work):
@@ -319,7 +347,12 @@
                 cot_live[
                     w * latent_count : (w + 1) * latent_count, m * quarter : (m + 1) * quarter
                 ] = (full[m, CHUNKS, w].astype(f32) * alive[w]).astype(bf16)
-        grad_attended[...] = dot(cot_live[...], out_weight_ref[...], (1, 1)).astype(bf16)
+        grad_attended = dot(cot_live[...], out_weight_ref[...], (1, 1)).astype(bf16)
+        for w in range(work):
+            wide = spread_heads(grad_attended[w * latent_count : (w + 1) * latent_count, :])
+            wide_grads[w] = wide.astype(bf16)
+            wide_grads_t[w] = wide.T.astype(bf16)
+            latent_slopes[w] = dot(latent_values, wide.astype(bf16), (1, 1))
 
     def finish(c):
         for copy in forward_arrivals(c):
@@ -329,6 +362,8 @@
         else:
             project(c)
 
+    pl.semaphore_wait(known_sems.at[0], 2)
+    greet(1, 4)
     order = [CHUNKS] + list(range(CHUNKS))
     for i, c in enumerate(order):
         if i < CHUNKS:
@@ -346,8 +381,8 @@
             finish(order[i - 1])
     finish(order[-1])
 
-    half_r = inner // 2
-    top, bottom = pl.ds(0, half_r), pl.ds(half_r, half_r)
+    half_r = inner // CORES
+    top, bottom = pl.ds(0, half_r // 2), pl.ds(half_r // 2, half_r // 2)
     y_copies = [
         remote(partial.at[y_far, low], y_relay.at[0], y_sems, 0, me_d, y_right),
         remote(partial.at[y_far, high], y_relay.at[1], y_sems, 1, me_d, y_left),
@@ -356,127 +391,165 @@
         remote(y_sum.at[0], y_got.at[0, low], y_sems, 4, me_d, y_right),
         remote(y_sum.at[1], y_got.at[1, high], y_sems, 5, me_d, y_left),
     ]
+    pl.semaphore_wait(known_sems.at[1], 2)
+    extent = tokens + latent_count
+    parts = []
     for w in range(work):
         begin = w * tokens
-        slot_keys = keys[begin : begin + tokens, :]
-        slot_values = values[begin : begin + tokens, :]
-        scores = dot(slot_keys, wide_queries, (1, 1)) * 0.125
+        slot_scores = scores[begin : begin + tokens, :]
         top_score = jnp.maximum(
-            jnp.max(scores, axis=0, keepdims=True), jnp.max(latent_scores, axis=0, keepdims=True)
+            jnp.max(slot_scores, axis=0, keepdims=True),
+            jnp.max(latent_scores, axis=0, keepdims=True),
         )
-        weight = jnp.exp(scores - top_score)
+        weight = jnp.exp(slot_scores - top_score)
         latent_weight = jnp.exp(latent_scores - top_score)
         total = jnp.sum(weight, axis=0, keepdims=True) + jnp.sum(
             latent_weight, axis=0, keepdims=True
         )
-        attention = weight / total
-        latent_attention = latent_weight / total
-        attention_b = attention.astype(bf16)
-        latent_attention_b = latent_attention.astype(bf16)
-        attended = dot(attention_b, slot_values, (0, 0)) + dot(
-            latent_attention_b, latent_values, (0, 0)
+        inverse_total = 1.0 / total
+        weight = weight * inverse_total
+        latent_weight = latent_weight * inverse_total
+        attention[w, 0:tokens, :] = weight
+        attention[w, tokens:extent, :] = latent_weight
+        weight = weight.astype(bf16)
+        latent_weight = latent_weight.astype(bf16)
+        attended = dot(weight, values[begin : begin + tokens, :], (0, 0)) + dot(
+            latent_weight, latent_values, (0, 0)
         )
         attended = jnp.where(same_head, attended, 0.0)
-        attended = sum(
-            attended[h * latent_count : (h + 1) * latent_count, :] for h in range(heads)
+        parts.append(
+            sum(
+                attended[h * latent_count : (h + 1) * latent_count, :] for h in range(heads)
+            ).astype(bf16)
+        )
+        where = work * tokens + w * latent_count
+        grads[inner : 2 * inner, begin : begin + tokens] = dot(
+            wide_grads_t[w], weight, (1, 1)
         ).astype(bf16)
-        part = dot(attended, out_weight_ref[...]).astype(bf16)
+        grads[inner : 2 * inner, where : where + latent_count] = dot(
+            wide_grads_t[w], latent_weight, (1, 1)
+        ).astype(bf16)
+    part = dot(jnp.concatenate(parts, axis=0), out_weight_ref[...]).astype(bf16)
+    for w in range(work):
         for m in range(n_mp):
-            partial[m, w] = part[:, m * quarter : (m + 1) * quarter]
-        if w == half_w - 1:
-            y_copies[0].start()
-            y_copies[3].start()
-        if w == work - 1:
-            y_copies[1].start()
-            y_copies[2].start()
-
-        slot_grad = grad_attended[w * latent_count : (w + 1) * latent_count, :]
-        wide_grad32 = spread_heads(slot_grad)
-        wide_grad = wide_grad32.astype(bf16)
-        wide_grad_t = wide_grad32.T.astype(bf16)
-        slope = dot(slot_values, wide_grad, (1, 1))
-        latent_slope = dot(latent_values, wide_grad, (1, 1))
-        row_dot = jnp.sum(attention * slope, axis=0, keepdims=True) + jnp.sum(
-            latent_attention * latent_slope, axis=0, keepdims=True
+            partial[m, w] = part[
+                w * latent_count : (w + 1) * latent_count, m * quarter : (m + 1) * quarter
+            ]
+    for i in range(4):
+        y_copies[i].start()
+
+    def x_copies_of(kind):
+        moves = (
+            (x_far, top, x_relay.at[kind, 0], dp_right),
+            (x_far, bottom, x_relay.at[kind, 1], dp_left),
+            (x_right, bottom, x_got.at[kind, 0, bottom], dp_right),
+            (x_left, top, x_got.at[kind, 1, top], dp_left),
+            (x_right, top, x_got.at[kind, 0, top], dp_right),
+            (x_left, bottom, x_got.at[kind, 1, bottom], dp_left),
         )
-        for where, count, att, att_b, slopes in (
-            (begin, tokens, attention, attention_b, slope),
-            (
-                work * tokens + w * latent_count,
-                latent_count,
-                latent_attention,
-                latent_attention_b,
-                latent_slope,
-            ),
+        return [
+            remote(x_sum.at[kind, x, part_rows], dst, x_sems, 6 * kind + i, d, me_m)
+            for i, (x, part_rows, dst, d) in enumerate(moves)
+        ]
+
+    x_order = (x_far, x_right, x_left, me_x)
+    x_copies = [x_copies_of(kind) for kind in range(2)]
+    core_copies = [
+        [
+            remote(
+                core_both.at[kind, i, other],
+                core_got.at[kind, i],
+                core_sems,
+                n_x * kind + i,
+                dp_other,
+                me_m,
+            )
+            for i in range(n_x)
+        ]
+        for kind in range(2)
+    ]
+    inverse = 1.0 / (n_dp * work)
+
+    def join_cores(kind, i):
+        core_copies[kind][i].wait_recv()
+        x_sum[kind, x_order[i]] = (
+            core_both[kind, i, me_core].astype(f32) + core_got[kind, i].astype(f32)
+        ).astype(bf16)
+        if i == 0:
+            x_copies[kind][0].start()
+            x_copies[kind][1].start()
+        elif i < 3:
+            x_copies[kind][i + 1].start()
+
+    def weight_grads(kind):
+        for i, x in enumerate(x_order):
+            product = dot(grads[kind * inner : (kind + 1) * inner, :], context[x]) * inverse
+            for core in range(CORES):
+                core_both[kind, i, core] = product[core * half_r : (core + 1) * half_r, :].astype(
+                    bf16
+                )
+            core_copies[kind][i].start()
+            if i > 0:
+                join_cores(kind, i - 1)
+
+    def relay_x(kind):
+        x_copies[kind][0].wait_recv()
+        x_sum[kind, x_right, top] = (
+            x_sum[kind, x_right, top].astype(f32) + x_relay[kind, 0].astype(f32)
+        ).astype(bf16)
+        x_copies[kind][4].start()
+        x_copies[kind][1].wait_recv()
+        x_sum[kind, x_left, bottom] = (
+            x_sum[kind, x_left, bottom].astype(f32) + x_relay[kind, 1].astype(f32)
+        ).astype(bf16)
+        x_copies[kind][5].start()
+
+    def finish_x(kind):
+        for i in range(2, 6):
+            x_copies[kind][i].wait_recv()
+        own = x_sum[kind, me_x].astype(f32)
+        return (own + x_got[kind, 0].astype(f32) + x_got[kind, 1].astype(f32)).T
+
+    def key_gradient(w):
+        where = work * tokens + w * latent_count
+        slope, latent_slope = slopes[w * tokens : (w + 1) * tokens, :], latent_slopes[w]
+        weight, latent_weight = attention[w, 0:tokens, :], attention[w, tokens:extent, :]
+        row_dot = jnp.sum(weight * slope, axis=0, keepdims=True) + jnp.sum(
+            latent_weight * latent_slope, axis=0, keepdims=True
+        )
+        for begin, count, share_of, slope_of in (
+            (w * tokens, tokens, weight, slope),
+            (where, latent_count, latent_weight, latent_slope),
         ):
-            grad_scores = att * (slopes - row_dot)
+            grad_scores = share_of * (slope_of - row_dot)
             near = grad_scores.astype(bf16)
             rest = (grad_scores - near.astype(f32)).astype(bf16)
-            grad_keys = (
-                dot(wide_queries_t, near, (1, 1)) + dot(wide_queries_t, rest, (1, 1))
-            ) * 0.125
-            grads[0:inner, where : where + count] = grad_keys.astype(bf16)
-            grads[inner : 2 * inner, where : where + count] = dot(
-                wide_grad_t, att_b, (1, 1)
+            grads[0:inner, begin : begin + count] = (
+                (dot(wide_queries_t, near, (1, 1)) + dot(wide_queries_t, rest, (1, 1))) * 0.125
             ).astype(bf16)
 
-    x_copies = [
-        remote(x_sum.at[x_far, top], x_relay.at[0], x_sems, 0, dp_right, me_m),
-        remote(x_sum.at[x_far, bottom], x_relay.at[1], x_sems, 1, dp_left, me_m),
-        remote(x_sum.at[x_right, bottom], x_got.at[0, bottom], x_sems, 2, dp_right, me_m),
-        remote(x_sum.at[x_left, top], x_got.at[1, top], x_sems, 3, dp_left, me_m),
-        remote(x_sum.at[x_right, top], x_got.at[0, top], x_sems, 4, dp_right, me_m),
-        remote(x_sum.at[x_left, bottom], x_got.at[1, bottom], x_sems, 5, dp_left, me_m),
-    ]
-    x_order = (x_far, x_right, x_left, me_x)
-    core_copies = [
-        remote(core_send.at[i], core_got.at[i], core_sems, i, dp_other, me_m) for i in range(n_x)
-    ]
-    inverse = 1.0 / (n_dp * work)
-
-    def weight_grad(kind, x):
-        left_side = grads[pl.ds(pl.multiple_of(kind * inner, inner), inner), :]
-        right_side = context[:, pl.ds(pl.multiple_of(x * quarter, 128), quarter)]
-        return dot(left_side, right_side) * inverse
-
-    def join_cores(i):
-        core_copies[i].wait_recv()
-        x_sum[x_order[i]] = (x_own[i] + core_got[i].astype(f32)).astype(bf16)
-        if i == 0:
-            x_copies[0].start()
-            x_copies[1].start()
-        elif i < 3:
-            x_copies[i + 1].start()
-
-    for i, x in enumerate(x_order):
-        core_send[i] = weight_grad(other, x).astype(bf16)
-        core_copies[i].start()
-        x_own[i] = weight_grad(me_core, x)
-        if i > 0:
-            join_cores(i - 1)
-
+    weight_grads(1)
+    for w in range(half_w):
+        key_gradient(w)
+    join_cores(1, n_x - 1)
     y_copies[0].wait_recv()
     y_sum[0] = (partial[y_right, low].astype(f32) + y_relay[0].astype(f32)).astype(bf16)
     y_copies[4].start()
     y_copies[1].wait_recv()
     y_sum[1] = (partial[y_left, high].astype(f32) + y_relay[1].astype(f32)).astype(bf16)
     y_copies[5].start()
-    join_cores(n_x - 1)
-    x_copies[0].wait_recv()
-    x_sum[x_right, top] = (x_sum[x_right, top].astype(f32) + x_relay[0].astype(f32)).astype(bf16)
-    x_copies[4].start()
-    x_copies[1].wait_recv()
-    x_sum[x_left, bottom] = (x_sum[x_left, bottom].astype(f32) + x_relay[1].astype(f32)).astype(
-        bf16
-    )
-    x_copies[5].start()
-    for i in range(2, 6):
-        x_copies[i].wait_recv()
-    summed = (x_sum[me_x].astype(f32) + x_got[0].astype(f32) + x_got[1].astype(f32)).T
+    for w in range(half_w, work):
+        key_gradient(w)
+    relay_x(1)
+    weight_grads(0)
+    join_cores(0, n_x - 1)
+    summed_values = finish_x(1)
+    relay_x(0)
+    summed_keys = finish_x(0)
     share = quarter // DEPTH
     for z in range(DEPTH):
-        piece = summed[z * share : (z + 1) * share, :]
-        z_send[z] = jnp.concatenate([piece[:, :128], piece[:, 128:]], axis=0).astype(bf16)
+        its = slice(z * share, (z + 1) * share)
+        z_send[z] = jnp.concatenate([summed_keys[its], summed_values[its]], axis=0).astype(bf16)
     z_copies = {
         o: remote(
             z_send.at[z_of(o)],
@@ -510,17 +583,32 @@
     first_core = me_core == 0
     ours, theirs = last[...], last_got[...]
     each = share // CORES
-    for out, block in (
-        (key_ref, jnp.where(first_core, ours, theirs)),
-        (value_ref, jnp.where(first_core, theirs, ours)),
+    for core, block in enumerate(
+        (jnp.where(first_core, ours, theirs), jnp.where(first_core, theirs, ours))
     ):
-        for half in range(2):
-            piece = block[half * share : (half + 1) * share, :]
-            out[:, half * 128 : (half + 1) * 128] = jnp.where(
+        for kind, out in enumerate((key_ref, value_ref)):
+            piece = block[kind * share : (kind + 1) * share, :]
+            out[:, core * 128 : (core + 1) * 128] = jnp.where(
                 first_core, piece[:each, :], piece[each:, :]
             )
-    for copy in started + y_copies + x_copies + core_copies + list(z_copies.values()) + [last_copy]:
+    started += y_copies + list(z_copies.values()) + [last_copy]
+    for kind in range(2):
+        started += x_copies[kind] + core_copies[kind]
+    for copy in started:
         copy.wait_send()
+
+
+def hand_over(*refs):
+    sources, results, held, sems = refs[:3], refs[3:6], refs[6:9], refs[9]
+    taken = [pltpu.make_async_copy(sources[i], held[i], sems.at[0, i]) for i in range(3)]
+    given = [pltpu.make_async_copy(held[i], results[i], sems.at[1, i]) for i in range(3)]
+    for copy in taken:
+        copy.start()
+    for first, second in zip(taken, given):
+        first.wait()
+        second.start()
+    for copy in given:
+        copy.wait()
 
 
 def local(
@@ -543,6 +631,8 @@
     rows = tokens // CHUNKS
     n_x = n_dp // (DEPTH * CORES)
     share = quarter // DEPTH
+    each = inner // CORES
+    wide = inner // HEAD * latent_count
     context_rows = work * (tokens + latent_count)
     half = (2, work // 2, latent_count, quarter)
     f32, bf16 = jnp.float32, jnp.bfloat16
@@ -553,7 +643,7 @@
     def like(x):
         return pltpu.VMEM(x.shape, x.dtype)
 
-    return pl.pallas_call(
+    results = pl.pallas_call(
         functools.partial(body, n_dp, n_mp),
         name="resample",
         out_shape=(
@@ -578,22 +668,25 @@
             pltpu.VMEM((CHUNKS, REACH, rows, quarter), bf16),
             pltpu.VMEM((REACH, 16, quarter), bf16),
             pltpu.VMEM((n_mp, CHUNKS + 1, work, rows, quarter), bf16),
-            pltpu.VMEM((context_rows, width), bf16),
+            pltpu.VMEM((n_mp, context_rows, quarter), bf16),
             pltpu.VMEM((work * latent_count, width), bf16),
             pltpu.VMEM((work * tokens, inner), bf16),
-            pltpu.VMEM((work * tokens, inner), bf16),
-            pltpu.VMEM((work * latent_count, inner), bf16),
+            pltpu.VMEM((work * tokens, wide), f32),
+            pltpu.VMEM((work * tokens, wide), f32),
+            pltpu.VMEM((work, latent_count, wide), f32),
+            pltpu.VMEM((work, wide, inner), bf16),
+            pltpu.VMEM((work, inner, wide), bf16),
+            pltpu.VMEM((work, tokens + latent_count, wide), f32),
             pltpu.VMEM((2 * inner, context_rows), bf16),
             pltpu.VMEM((n_mp, work, latent_count, quarter), bf16),
             pltpu.VMEM(half, bf16),
             pltpu.VMEM(half, bf16),
             pltpu.VMEM((2, work, latent_count, quarter), bf16),
-            pltpu.VMEM((n_x, inner, quarter), bf16),
-            pltpu.VMEM((n_x, inner, quarter), bf16),
-            pltpu.VMEM((n_x, inner, quarter), f32),
-            pltpu.VMEM((n_x, inner, quarter), bf16),
-            pltpu.VMEM((2, inner // 2, quarter), bf16),
-            pltpu.VMEM((2, inner, quarter), bf16),
+            pltpu.VMEM((2, n_x, CORES, each, quarter), bf16),
+            pltpu.VMEM((2, n_x, each, quarter), bf16),
+            pltpu.VMEM((2, n_x, each, quarter), bf16),
+            pltpu.VMEM((2, 2, each // 2, quarter), bf16),
+            pltpu.VMEM((2, 2, each, quarter), bf16),
             pltpu.VMEM((DEPTH, 2 * share, 128), bf16),
             pltpu.VMEM((DEPTH - 1, 2 * share, 128), bf16),
             pltpu.VMEM((2 * share, 128), f32),
@@ -603,10 +696,11 @@
             dma((2, REACH)),
             dma((2, 4 * CHUNKS + 4)),
             dma((2, 6)),
-            dma((2, n_x)),
-            dma((2, 6)),
+            dma((2, 2 * n_x)),
+            dma((2, 12)),
             dma((2, DEPTH - 1)),
             dma((2, 1)),
+            pltpu.SemaphoreType.REGULAR((2,)),
         ],
         compiler_params=pltpu.CompilerParams(
             collective_id=0, has_side_effects=True, vmem_limit_bytes=60 << 20
@@ -623,6 +717,15 @@
         value_weight,
         out_weight,
     )
+    return pl.pallas_call(
+        hand_over,
+        name="hand_over",
+        out_shape=tuple(jax.ShapeDtypeStruct(r.shape, r.dtype) for r in results),
+        in_specs=[hbm] * 3,
+        out_specs=(hbm,) * 3,
+        scratch_shapes=[like(r) for r in results] + [dma((2, 3))],
+        compiler_params=pltpu.CompilerParams(vmem_limit_bytes=60 << 20),
+    )(*results)
 
 
 def solution(mesh):

time: 94.7 us -> 87.2 us (0.921)
  local copies, waits for them, and re-layouts: 4.27 us -> 0 us
  Pallas kernels: 89.5 us -> 86.2 us
    pallas_call x1, Pallas kernels: 89.5 us -> 84.6 us  [local(): pl.pallas_call(functools.partial(body, n_dp, n_mp), name='resample', out_...]
    unnamed x3 -> x0, local copies, waits for them, and re-layouts: 4.27 us -> none
    pallas_call x0 -> x1, Pallas kernels: none -> 1.66 us  [local(): pl.pallas_call(hand_over, name='hand_over', out_shape=tuple((jax.ShapeDty...]
where the time goes in v4:
time: 87.2 us; the launch traced here: 87 us
  Pallas kernels  86.2 us (99%)
    pallas_call x1, Pallas kernels, local(): pl.pallas_call(functools.partial(body, n_dp, n_mp), name='resample', out_...  84.6 us

profile of v4, /device:TPU:1, one launch (start us, length us, event | category | flops | bytes accessed | tf_op | source)
XLA Modules:
  0.0 87.0 jit_solution(2150355998368052893)
XLA Ops:
  0.6 84.6 %resample.1 = (bf16[4,64,384]{2,1,0:T(8,128)(2,1)}, f32[12,256]{1,0:T(8,128)}, f32[12,256]{1,0:T(8,128)}) custom-call(s32[1,8]{1,0:T(1,128)} %plan_hbm.1, s32[2]{0:T(128)} %docs_hbm.1, bf16[8,384]{1,0:T(8,128)(2,1)} %time_hbm.1, bf16[8,256,384]{2,1,0:T(8,128)(2,1)} %media_hbm.1, bf16[4,64,384]{2,1,0:T(8,128)(2,1)} %cot_hbm.1, bf16[64,256]{1,0:T(8,128)(2,1)} %queries_hbm.1, ...), custom_call_target="tpu_custom_call" | custom-call | tf_op jit(solution)/shard_map/resample/pallas_call | solution.py:646
  85.2 1.7 %hand_over.1 = (bf16[4,64,384]{2,1,0:T(8,128)(2,1)}, f32[12,256]{1,0:T(8,128)}, f32[12,256]{1,0:T(8,128)}) custom-call(bf16[4,64,384]{2,1,0:T(8,128)(2,1)} %get-tuple-element.6.refs_0_, f32[12,256]{1,0:T(8,128)} %get-tuple-element.7.refs_1_, f32[12,256]{1,0:T(8,128)} %get-tuple-element.8.refs_2_), custom_call_target="tpu_custom_call" | custom-call | tf_op jit(solution)/shard_map/hand_over/pallas_call | solution.py:720

commit v5 on v4

--- a/solution.py
+++ b/solution.py
@@ -541,28 +541,44 @@
     for w in range(half_w, work):
         key_gradient(w)
     relay_x(1)
+    share = quarter // DEPTH
+    far_first = sorted(range(1, DEPTH), key=lambda o: -min(o, DEPTH - o))
+    z_copies = [
+        {
+            o: remote(
+                z_send.at[kind, z_of(o)],
+                z_got.at[kind, o - 1],
+                z_sems,
+                kind * (DEPTH - 1) + o - 1,
+                at(me_x, z_of(o), me_core),
+                me_m,
+            )
+            for o in range(1, DEPTH)
+        }
+        for kind in range(2)
+    ]
+
+    def start_z(kind):
+        summed = finish_x(kind)
+        for z in range(DEPTH):
+            z_send[kind, z] = summed[z * share : (z + 1) * share, :].astype(bf16)
+        for o in far_first:
+            z_copies[kind][o].start()
+
     weight_grads(0)
+    start_z(1)
+    relay_x(0)
     join_cores(0, n_x - 1)
-    summed_values = finish_x(1)
-    relay_x(0)
-    summed_keys = finish_x(0)
-    share = quarter // DEPTH
-    for z in range(DEPTH):
-        its = slice(z * share, (z + 1) * share)
-        z_send[z] = jnp.concatenate([summed_keys[its], summed_values[its]], axis=0).astype(bf16)
-    z_copies = {
-        o: remote(
-            z_send.at[z_of(o)],
-            z_got.at[o - 1],
-            z_sems,
-            o - 1,
-            at(me_x, z_of(o), me_core),
-            me_m,
-        )
-        for o in range(1, DEPTH)
-    }
-    for o in sorted(range(1, DEPTH), key=lambda o: -min(o, DEPTH - o)):
-        z_copies[o].start()
+    start_z(0)
+
+    for kind in (1, 0):
+        total = z_send[kind, me_z].astype(f32)
+        for o in reversed(far_first):
+            z_copies[kind][o].wait_recv()
+            total = total + z_got[kind, o - 1].astype(f32)
+        last[kind * share : (kind + 1) * share, :] = total
+    last_copy = remote(last, last_got, last_sems, 0, dp_other, me_m)
+    last_copy.start()
 
     for i in range(2, 6):
         y_copies[i].wait_recv()
@@ -572,13 +588,6 @@
         heads_sum = heads_sum + y_got[1, w].astype(f32)
         resampled_ref[w] = ((mine + heads_sum) * alive[w]).astype(bf16)
 
-    total = z_send[me_z].astype(f32)
-    for o in sorted(range(1, DEPTH), key=lambda o: min(o, DEPTH - o)):
-        z_copies[o].wait_recv()
-        total = total + z_got[o - 1].astype(f32)
-    last[...] = total
-    last_copy = remote(last, last_got, last_sems, 0, dp_other, me_m)
-    last_copy.start()
     last_copy.wait_recv()
     first_core = me_core == 0
     ours, theirs = last[...], last_got[...]
@@ -591,9 +600,9 @@
             out[:, core * 128 : (core + 1) * 128] = jnp.where(
                 first_core, piece[:each, :], piece[each:, :]
             )
-    started += y_copies + list(z_copies.values()) + [last_copy]
+    started += y_copies + [last_copy]
     for kind in range(2):
-        started += x_copies[kind] + core_copies[kind]
+        started += x_copies[kind] + core_copies[kind] + list(z_copies[kind].values())
     for copy in started:
         copy.wait_send()
 
@@ -687,8 +696,8 @@
             pltpu.VMEM((2, n_x, each, quarter), bf16),
             pltpu.VMEM((2, 2, each // 2, quarter), bf16),
             pltpu.VMEM((2, 2, each, quarter), bf16),
-            pltpu.VMEM((DEPTH, 2 * share, 128), bf16),
-            pltpu.VMEM((DEPTH - 1, 2 * share, 128), bf16),
+            pltpu.VMEM((2, DEPTH, share, 128), bf16),
+            pltpu.VMEM((2, DEPTH - 1, share, 128), bf16),
             pltpu.VMEM((2 * share, 128), f32),
             pltpu.VMEM((2 * share, 128), f32),
             dma((10,)),
@@ -698,7 +707,7 @@
             dma((2, 6)),
             dma((2, 2 * n_x)),
             dma((2, 12)),
-            dma((2, DEPTH - 1)),
+            dma((2, 2 * DEPTH - 2)),
             dma((2, 1)),
             pltpu.SemaphoreType.REGULAR((2,)),
         ],

time: 87.2 us -> 86.2 us (0.989)
  Pallas kernels: 86.2 us -> 85.2 us
    pallas_call x1, Pallas kernels: 84.6 us -> 83.6 us  [local(): pl.pallas_call(functools.partial(body, n_dp, n_mp), name='resample', out_...]
where the time goes in v5:
time: 86.2 us; the launch traced here: 86 us
  Pallas kernels  85.2 us (99%)
    pallas_call x1, Pallas kernels, local(): pl.pallas_call(functools.partial(body, n_dp, n_mp), name='resample', out_...  83.6 us

profile of v5, /device:TPU:1, one launch (start us, length us, event | category | flops | bytes accessed | tf_op | source)
XLA Modules:
  0.0 86.0 jit_solution(2410645337277985817)
XLA Ops:
  0.6 83.6 %resample.1 = (bf16[4,64,384]{2,1,0:T(8,128)(2,1)}, f32[12,256]{1,0:T(8,128)}, f32[12,256]{1,0:T(8,128)}) custom-call(s32[1,8]{1,0:T(1,128)} %plan_hbm.1, s32[2]{0:T(128)} %docs_hbm.1, bf16[8,384]{1,0:T(8,128)(2,1)} %time_hbm.1, bf16[8,256,384]{2,1,0:T(8,128)(2,1)} %media_hbm.1, bf16[4,64,384]{2,1,0:T(8,128)(2,1)} %cot_hbm.1, bf16[64,256]{1,0:T(8,128)(2,1)} %queries_hbm.1, ...), custom_call_target="tpu_custom_call" | custom-call | tf_op jit(solution)/shard_map/resample/pallas_call | solution.py:655
  84.2 1.7 %hand_over.1 = (bf16[4,64,384]{2,1,0:T(8,128)(2,1)}, f32[12,256]{1,0:T(8,128)}, f32[12,256]{1,0:T(8,128)}) custom-call(bf16[4,64,384]{2,1,0:T(8,128)(2,1)} %get-tuple-element.6.refs_0_, f32[12,256]{1,0:T(8,128)} %get-tuple-element.7.refs_1_, f32[12,256]{1,0:T(8,128)} %get-tuple-element.8.refs_2_), custom_call_target="tpu_custom_call" | custom-call | tf_op jit(solution)/shard_map/hand_over/pallas_call | solution.py:729
